TPU v7x, 32 devices: a whole 2x2x4 slice. The times are simulated.
32 devices in a mesh: groups: 2 (over y), ctx: 4 (over z), head: 2 (over x), sec: 2 (over core).
Axes of the slice: x: 2, y: 2, z: 4, core: 2. Of those that a mesh axis runs over, the one named last changes fastest.
Arguments:
- queries: bfloat16 [256, 8192], P(('groups', 'ctx'), ('head', 'sec')), parts along dimension 0, may hold values from -128 to 128
- key_cache: bfloat16 [16384, 1024], P(('groups', 'ctx'), ('head', 'sec')), parts along dimension 0, may hold values from -4.5 to 4.5
- value_cache: bfloat16 [16384, 1024], P(('groups', 'ctx'), ('head', 'sec')), parts along dimension 0, may hold values from -6 to 6
- block_index: int32 [2, 8], P('groups'), parts along dimension 0, may hold values from 0 to 63, as said below
- stream: bfloat16 [256, 8192], P(('groups', 'head', 'sec'), 'ctx'), parts along dimension 0, may hold values from -6 to 6
- out_weight: bfloat16 [8192, 8192], P(('head', 'sec'), 'ctx'), may hold values from -0.0625 to 0.0625
- norm_gain: float32 [8192], replicated, may hold values from 0.5 to 1.5
- gate_weight: bfloat16 [8192, 14336], P(('head', 'sec'), 'ctx'), may hold values from -0.0625 to 0.0625
- up_weight: bfloat16 [8192, 14336], P(('head', 'sec'), 'ctx'), may hold values from -0.0625 to 0.0625
- down_weight: bfloat16 [14336, 8192], P('ctx', ('head', 'sec')), may hold values from -0.046875 to 0.046875
Outputs:
- layer_out: bfloat16 [256, 8192], P(('groups', 'ctx'), ('head', 'sec')), parts along dimension 0
There are 2 independent parts, one for each index of `groups`. A program takes and returns all parts, laid end to end along the dimension named above; an argument that names none is the same for every part. Nothing has to cross between parts.
Inputs may be any that keep to these rules, and one draw needn't show every extreme that they name: `block_index`: row b lists 8 distinct key blocks in increasing order, none after the block 63 + b, and includes that block and block 0. Of the aligned runs of 16 key blocks (k * 16 to (k + 1) * 16 - 1), each holds at least one of a row's blocks and at most 4, and in every row some run holds exactly 4.
All inputs are finite; a program needn't handle non-finite values.
Results may differ from a plain program's by a relative error of at most 0.014.
Values may be sent and summed in bfloat16 or wider, within the bound.
No kernel may reach another device: no remote copies, remote signals or barrier semaphores. Data moves between devices by JAX's collectives and lax.ppermute only.
A program may use at most 128 MiB of HBM per device.

v0:
```python
import functools
import math

import jax
import jax.numpy as jnp
from jax import lax
from jax.experimental import pallas as pl
from jax.experimental.pallas import tpu as pltpu
from jax.sharding import PartitionSpec as P


HQ = 64
KVH = 8
DH = 128
KB = 128
MOST = 4
LANES = 128
EPS = 1e-05
ALL = ("ctx", "head", "sec")


VM = pl.BlockSpec(memory_space=pltpu.VMEM)
SM = pl.BlockSpec(memory_space=pltpu.SMEM)
ANY = pl.BlockSpec(memory_space=pl.ANY)
F32 = jnp.float32
BF16 = jnp.bfloat16


def struct(shape, dtype):
    return jax.ShapeDtypeStruct(shape, dtype)


def call(kernel, out, in_specs, args, cost=3, scratch=(), vmem=8):
    outs = out if isinstance(out, (tuple, list)) else (out,)
    nbytes = sum(math.prod(a.shape) * a.dtype.itemsize for a in args)
    nbytes += sum(math.prod(o.shape) * o.dtype.itemsize for o in outs)
    return pl.pallas_call(
        kernel,
        out_shape=out,
        in_specs=in_specs,
        out_specs=jax.tree.map(lambda _: VM, out),
        scratch_shapes=scratch,
        compiler_params=pltpu.CompilerParams(vmem_limit_bytes=vmem << 20),
        cost_estimate=pl.CostEstimate(flops=cost * 10**9, bytes_accessed=nbytes, transcendentals=0),
    )(*args)


def in_vmem(x):
    return pltpu.with_memory_space_constraint(x, pltpu.VMEM)


def in_hbm(x):
    return pltpu.with_memory_space_constraint(x, pltpu.HBM)


def slots(index_ref, shard, blocks):
    first = jnp.int32(0)
    count = jnp.int32(0)
    for n in range(index_ref.shape[1]):
        block = index_ref[0, n]
        first += (block < shard * blocks).astype(jnp.int32)
        count += (block < (shard + 1) * blocks).astype(jnp.int32)
    return first, count - first


def slot_block(index_ref, first, count, slot, shard, blocks):
    entry = jnp.minimum(first + slot, index_ref.shape[1] - 1)
    local = jnp.clip(index_ref[0, entry] - shard * blocks, 0, blocks - 1)
    return local, slot < count


def pick_kernel(index_ref, meta_ref, key_ref, value_ref, key_out, value_out, sems):
    blocks = key_ref.shape[0] // KB
    shard = meta_ref[0]
    first, count = slots(index_ref, shard, blocks)
    copies = []
    for slot in range(MOST):
        local, _ = slot_block(index_ref, first, count, slot, shard, blocks)
        rows = pl.ds(pl.multiple_of(local * KB, KB), KB)
        for n, (src, dst) in enumerate(((key_ref, key_out), (value_ref, value_out))):
            copy = pltpu.make_async_copy(
                src.at[rows, :], dst.at[slot * KB : (slot + 1) * KB, :], sems.at[n, slot]
            )
            copy.start()
            copies.append(copy)
    for copy in copies:
        copy.wait()


def attend_kernel(offset, blocks, context_len, total, index_ref, meta_ref, q_ref, key_ref, value_ref, out_ref):
    rows = q_ref.shape[0]
    heads = q_ref.shape[1] // DH
    kv_dev = key_ref.shape[1] // DH
    group = heads // kv_dev
    shard = meta_ref[0]
    token0 = context_len - total + (shard ^ offset) * rows
    first, count = slots(index_ref, shard, blocks)
    limits = []
    for slot in range(MOST):
        local, valid = slot_block(index_ref, first, count, slot, shard, blocks)
        limit = token0 - (shard * blocks + local) * KB
        limits.append(jnp.where(valid, limit, jnp.int32(-(1 << 20))))
    row = lax.broadcasted_iota(jnp.int32, (group * rows, KB), 0) % rows
    lane = lax.broadcasted_iota(jnp.int32, (group * rows, KB), 1)
    ahead = lane - row
    head_lane = lax.broadcasted_iota(jnp.int32, (rows, LANES), 1)
    lse_tile = jnp.zeros((rows, LANES), F32)
    for kv in range(kv_dev):
        stacked = jnp.concatenate(
            [q_ref[:, (kv * group + h) * DH : (kv * group + h + 1) * DH] for h in range(group)], axis=0
        )
        scores = lax.dot_general(
            stacked,
            key_ref[:, kv * DH : (kv + 1) * DH],
            (((1,), (1,)), ((), ())),
            preferred_element_type=F32,
        ) * (1.0 / math.sqrt(DH))
        parts = [
            jnp.where(ahead <= limits[slot], scores[:, slot * KB : (slot + 1) * KB], -1e30)
            for slot in range(MOST)
        ]
        peak = functools.reduce(jnp.maximum, parts)
        peak = jnp.max(peak, axis=1, keepdims=True)
        parts = [jnp.exp(p - peak) for p in parts]
        row_total = jnp.sum(functools.reduce(jnp.add, parts), axis=1, keepdims=True)
        weights = jnp.concatenate([p.astype(BF16) for p in parts], axis=1)
        mixture = jnp.dot(
            weights, value_ref[:, kv * DH : (kv + 1) * DH], preferred_element_type=F32
        )
        mixture = (mixture * (1.0 / row_total)).astype(BF16)
        lse = peak + jnp.log(row_total)
        for h in range(group):
            head = kv * group + h
            span = slice(h * rows, (h + 1) * rows)
            out_ref[:, head * DH : (head + 1) * DH] = mixture[span]
            lse_tile = jnp.where(head_lane == head, lse[span], lse_tile)
    high = lse_tile.astype(BF16).astype(F32)
    rest = lse_tile - high
    mid = rest.astype(BF16).astype(F32)
    low = rest - mid
    tile = high + pltpu.roll(mid, heads, 1) + pltpu.roll(low, 2 * heads, 1)
    out_ref[:, heads * DH :] = tile.astype(BF16)


def blend_kernel(*refs):
    out_ref = refs[-1]
    parts = refs[:-1]
    heads = out_ref.shape[1] // DH
    logs = []
    for part in parts:
        tile = part[:, heads * DH :].astype(F32)
        logs.append(
            tile + pltpu.roll(tile, LANES - heads, 1) + pltpu.roll(tile, LANES - 2 * heads, 1)
        )
    peak = functools.reduce(jnp.maximum, logs)
    shares = [jnp.exp(log - peak) for log in logs]
    total = functools.reduce(jnp.add, shares)
    shares = [share / total for share in shares]
    for head in range(heads):
        span = slice(head * DH, (head + 1) * DH)
        out_ref[:, span] = functools.reduce(
            jnp.add,
            [share[:, head : head + 1] * part[:, span].astype(F32) for share, part in zip(shares, parts)],
        ).astype(BF16)


def place_of(meta_ref, n_sec, n, rows, count):
    owner = meta_ref[0] ^ n
    other = ((owner % n_sec) != meta_ref[2]).astype(jnp.int32)
    return pl.multiple_of(other * (count // n_sec * rows) + owner // n_sec * rows, rows)


def product(rows_ref, weight_ref, source, keep_ref, send_ref, target, width, tile):
    half = rows_ref.shape[0] // 2
    for at in range(0, width, tile):
        size = min(tile, width - at)
        part = jnp.dot(
            rows_ref[...],
            weight_ref[:, source + at : source + at + size],
            preferred_element_type=F32,
        )
        keep_ref[:, target + at : target + at + size] = part[:half]
        send_ref[:, target + at : target + at + size] = part[half:].astype(BF16)


def project_kernel(n_sec, tile, meta_ref, *refs):
    pieces, (weight_ref, keep_ref, send_ref, rows_ref) = refs[:-4], refs[-4:]
    rows = pieces[0].shape[0]
    for n, piece in enumerate(pieces):
        rows_ref[pl.ds(place_of(meta_ref, n_sec, n, rows, len(pieces)), rows), :] = piece[...]
    product(rows_ref, weight_ref, 0, keep_ref, send_ref, 0, weight_ref.shape[1], tile)


def fold_kernel(width, meta_ref, keep_ref, got_ref, keep_out, send_out):
    rows = keep_out.shape[0]
    mine = pl.ds(pl.multiple_of(meta_ref[1] * rows, rows), rows)
    other = pl.ds(pl.multiple_of((1 - meta_ref[1]) * rows, rows), rows)
    keep_out[:, :width] = keep_ref[mine, :width] + got_ref[mine, :width].astype(F32)
    send_out[:, :width] = (keep_ref[other, :width] + got_ref[other, :width].astype(F32)).astype(BF16)
    if keep_ref.shape[1] > width:
        keep_out[:, width:] = keep_ref[mine, width:] + take_exact(got_ref[mine, width:])
        put_exact(send_out, slice(None), width, keep_ref[other, width:] + take_exact(got_ref[other, width:]))


def middle_kernel(stream_ref, keep_ref, got_ref, out_ref):
    out_ref[...] = (
        stream_ref[...].astype(F32) + (keep_ref[...] + got_ref[...].astype(F32))
    ).astype(BF16)


def put_exact(ref, rows, at, value):
    high = value.astype(BF16)
    ref[rows, at : at + LANES] = high
    ref[rows, at + LANES : at + 2 * LANES] = (value - high.astype(F32)).astype(BF16)


def take_exact(tile):
    return tile[:, :LANES].astype(F32) + tile[:, LANES:].astype(F32)


def gate_kernel(n_sec, start, width, tile, with_norm, meta_ref, *refs):
    pieces = refs[:4]
    gain_ref, gate_ref, up_ref, keep_ref, send_ref, rows_ref = refs[4:]
    rows = pieces[0].shape[0]
    half = rows_ref.shape[0] // 2
    model = rows_ref.shape[1]
    gain = gain_ref[:, pl.ds(pl.multiple_of(meta_ref[3] * model, model), model)]
    for n, piece in enumerate(pieces):
        wide = piece[...].astype(F32)
        at = place_of(meta_ref, n_sec, n, rows, len(pieces))
        rows_ref[pl.ds(at, rows), :] = (wide * gain).astype(BF16)
        if with_norm:
            square = jnp.broadcast_to(jnp.sum(wide * wide, axis=1, keepdims=True), (rows, LANES))

            @pl.when(at < half)
            def _():
                keep_ref[pl.ds(at, rows), 2 * width :] = square

            @pl.when(at >= half)
            def _():
                put_exact(send_ref, pl.ds(pl.multiple_of(at - half, rows), rows), 2 * width, square)

    product(rows_ref, gate_ref, start, keep_ref, send_ref, 0, width, tile)
    product(rows_ref, up_ref, start, keep_ref, send_ref, width, width, tile)


def scale_kernel(model, keep_ref, got_ref, out_ref):
    at = keep_ref.shape[1] - LANES
    square = keep_ref[:, at:] + take_exact(got_ref[:, at:])
    out_ref[...] = lax.rsqrt(square / model + EPS)


def hidden_kernel(scale_ref, keep_ref, got_ref, out_ref):
    width = out_ref.shape[1]
    scale = scale_ref[...]
    for at in range(0, width, LANES):
        gate = keep_ref[:, at : at + LANES] + got_ref[:, at : at + LANES].astype(F32)
        up = keep_ref[:, width + at : width + at + LANES] + got_ref[
            :, width + at : width + at + LANES
        ].astype(F32)
        gate = gate * scale
        out_ref[:, at : at + LANES] = (
            gate / (1.0 + jnp.exp(-gate)) * (up * scale)
        ).astype(BF16)


def first_hidden_kernel(model, keep_ref, got_ref, out_ref, scale_ref):
    scale_kernel(model, keep_ref, got_ref, scale_ref)
    hidden_kernel(scale_ref, keep_ref, got_ref, out_ref)


def down_kernel(n_chunk, tile, meta_ref, *refs):
    pieces = refs[: 4 * n_chunk]
    weight_ref, own_ref = refs[4 * n_chunk : 4 * n_chunk + 2]
    sends, rows_ref = refs[4 * n_chunk + 2 : -1], refs[-1]
    rows = pieces[0].shape[0]
    shard, place = meta_ref[0], meta_ref[3]
    for n in range(4):
        at = pl.ds(pl.multiple_of((shard ^ place ^ n) * rows, rows), rows)
        start = 0
        for c in range(n_chunk):
            piece = pieces[n * n_chunk + c]
            rows_ref[at, start : start + piece.shape[1]] = piece[...]
            start += piece.shape[1]

    for at in range(0, weight_ref.shape[1], tile):
        columns = slice(at, at + tile)
        part = jnp.dot(rows_ref[...], weight_ref[:, columns], preferred_element_type=F32)
        own_ref[:, columns] = part[:rows]
        for n, send in enumerate(sends):
            send[:, columns] = part[(n + 1) * rows : (n + 2) * rows].astype(BF16)


def final_kernel(middle_ref, own_ref, *refs):
    parts, out_ref = refs[:-1], refs[-1]
    total = own_ref[...]
    for part in parts:
        total = total + part[...].astype(F32)
    out_ref[...] = (middle_ref[...].astype(F32) + total).astype(BF16)


def swap(x, axis):
    return lax.ppermute(x, axis, [(0, 1), (1, 0)])


def turn(x, axis, n, offset):
    return lax.ppermute(x, axis, [(i, i ^ offset) for i in range(n)])


def direct_body(
    queries,
    key_cache,
    value_cache,
    block_index,
    stream,
    out_weight,
    norm_gain,
    gate_weight,
    up_weight,
    down_weight,
):
    n_context, n_head, n_sec = (lax.axis_size(a) for a in ALL)
    shard, head, sec = (lax.axis_index(a) for a in ALL)
    place = head * n_sec + sec
    meta = jnp.stack([shard, head, sec, place]).astype(jnp.int32)
    rows, heads_width = queries.shape
    context_len = key_cache.shape[0] * n_context
    model = norm_gain.shape[0]
    total = rows * n_context
    blocks = key_cache.shape[0] // KB
    kv_width = key_cache.shape[1]
    order = (3, 1, 2)

    got_q = {m: turn(queries, "ctx", n_context, m) for m in order}
    got_q[0] = queries
    picked = struct((MOST * KB, kv_width), BF16)
    keys, values = call(
        pick_kernel,
        (picked, picked),
        [SM, SM, ANY, ANY],
        (block_index, meta, in_hbm(key_cache), in_hbm(value_cache)),
        scratch=[pltpu.SemaphoreType.DMA((2, MOST))],
    )
    partial = {}
    for m in (0,) + order:
        partial[m] = call(
            functools.partial(attend_kernel, m, blocks, context_len, total),
            struct((rows, heads_width + LANES), BF16),
            [SM, SM, VM, VM, VM],
            (block_index, meta, got_q[m], keys, values),
        )
    back = {m: turn(partial[m], "ctx", n_context, m) for m in order}
    back[0] = partial[0]
    blended = call(
        blend_kernel, struct((rows, heads_width), BF16), [VM] * 4, tuple(back[m] for m in range(4))
    )

    attention = {m: turn(blended, "ctx", n_context, m) for m in order}
    attention[0] = blended
    width = out_weight.shape[1]
    keep, away = call(
        functools.partial(project_kernel, n_sec, 512),
        (struct((n_head * rows, width), F32), struct((n_head * rows, width), BF16)),
        [SM] + [VM] * 5,
        (meta,) + tuple(attention[m] for m in range(4)) + (in_vmem(out_weight),),
        scratch=[pltpu.VMEM((total, heads_width), BF16)],
    )
    got = swap(away, "sec")
    keep, away = call(
        functools.partial(fold_kernel, width),
        (struct((rows, width), F32), struct((rows, width), BF16)),
        [SM, VM, VM],
        (meta, keep, got),
        cost=6,
    )
    got = swap(away, "head")
    middle = call(middle_kernel, struct((rows, width), BF16), [VM] * 3, (stream, keep, got), cost=6)

    all_middle = {
        m: lax.ppermute(
            middle,
            ALL,
            [
                (a * n_context + b, (b ^ m) * n_context + a)
                for a in range(n_context)
                for b in range(n_context)
            ],
        )
        for m in (3, 0, 1, 2)
    }
    hidden_width = gate_weight.shape[1]
    units = hidden_width // LANES
    first = units * 2 // 5 * LANES
    chunks = ((0, first), (first, hidden_width - first))
    hidden = []
    gate_vmem, up_vmem = in_vmem(gate_weight), in_vmem(up_weight)
    scale = None
    for c, (start, chunk) in enumerate(chunks):
        extra = LANES if c == 0 else 0
        keep, away = call(
            functools.partial(gate_kernel, n_sec, start, chunk, 256, c == 0),
            (
                struct((n_head * rows, 2 * chunk + extra), F32),
                struct((n_head * rows, 2 * chunk + 2 * extra), BF16),
            ),
            [SM] + [VM] * 7,
            (meta,) + tuple(all_middle[m] for m in range(4)) + (norm_gain[None], gate_vmem, up_vmem),
            scratch=[pltpu.VMEM((total, width), BF16)],
        )
        keep, away = call(
            functools.partial(fold_kernel, 2 * chunk),
            (
                struct((rows, 2 * chunk + extra), F32),
                struct((rows, 2 * chunk + 2 * extra), BF16),
            ),
            [SM, VM, VM],
            (meta, keep, swap(away, "sec")),
        )
        got = swap(away, "head")
        if c == 0:
            own, scale = call(
                functools.partial(first_hidden_kernel, model),
                (struct((rows, chunk), BF16), struct((rows, LANES), F32)),
                [VM] * 2,
                (keep, got),
            )
        else:
            own = call(hidden_kernel, struct((rows, chunk), BF16), [VM] * 3, (scale, keep, got))
        across = swap(own, "head")
        beside = swap(own, "sec")
        hidden.append((own, beside, across, swap(across, "sec")))
    n_chunk = len(chunks)

    out_width = down_weight.shape[1]
    res = call(
        functools.partial(down_kernel, n_chunk, 512),
        (struct((rows, out_width), F32),) + (struct((rows, out_width), BF16),) * 3,
        [SM] + [VM] * (4 * n_chunk + 1),
        (meta,)
        + tuple(hidden[c][n] for n in range(4) for c in range(n_chunk))
        + (in_vmem(down_weight),),
        scratch=[pltpu.VMEM((total, hidden_width), BF16)],
    )
    parts = [turn(res[m], "ctx", n_context, m) for m in order]
    return call(
        final_kernel, struct((rows, out_width), BF16), [VM] * 5, (all_middle[0], res[0]) + tuple(parts)
    )


def local_attention(gathered, key_cache, value_cache, block_index, context_index, context_len):
    group_size = HQ // KVH
    kv_dev = key_cache.shape[1] // DH
    blocks_dev = key_cache.shape[0] // KB
    total_tokens = gathered.shape[0]
    key_blocks = key_cache.reshape(blocks_dev, KB, kv_dev, DH)
    value_blocks = value_cache.reshape(blocks_dev, KB, kv_dev, DH)
    local_ids = context_index * blocks_dev + jnp.arange(blocks_dev, dtype=jnp.int32)
    member = jnp.any(block_index[:, :, None] == local_ids[None, None, :], axis=1)
    member_rank = jnp.cumsum(member.astype(jnp.int32), axis=1) - 1
    slot_hit = member[:, None, :] & (
        member_rank[:, None, :] == jnp.arange(MOST, dtype=jnp.int32)[None, :, None]
    )
    slot_block = jnp.sum(
        jnp.where(slot_hit, jnp.arange(blocks_dev, dtype=jnp.int32)[None, None, :], 0), axis=2
    )
    slot_valid = jnp.any(slot_hit, axis=2)
    picked_keys = jnp.take(key_blocks, slot_block[0], axis=0).reshape(MOST * KB, kv_dev, DH)
    picked_values = jnp.take(value_blocks, slot_block[0], axis=0).reshape(MOST * KB, kv_dev, DH)
    key_pos = (
        (local_ids[0] + slot_block[0])[:, None] * KB + jnp.arange(KB, dtype=jnp.int32)[None, :]
    ).reshape(-1)
    live_keys = jnp.broadcast_to(slot_valid[0][:, None], (MOST, KB)).reshape(-1)
    query_pos = context_len - total_tokens + jnp.arange(KB, dtype=jnp.int32)
    allowed = live_keys[None, :] & (key_pos[None, :] <= query_pos[:, None])
    query_block = gathered.reshape(KB, kv_dev, group_size, DH)
    scores = jnp.einsum(
        "qhgd,phd->hgqp", query_block, picked_keys, preferred_element_type=jnp.float32
    ) / math.sqrt(DH)
    scores = jnp.where(allowed[None, None], scores, -jnp.inf)
    peak_score = jnp.max(scores, axis=-1, keepdims=True)
    unnormed = jnp.exp(scores - peak_score)
    row_total = jnp.sum(unnormed, axis=-1)
    mixture = jnp.einsum(
        "hgqp,phd->qhgd",
        unnormed.astype(jnp.bfloat16),
        picked_values,
        preferred_element_type=jnp.float32,
    )
    result = mixture / jnp.transpose(row_total, (2, 0, 1))[..., None]
    log_total = jnp.transpose(peak_score[..., 0] + jnp.log(row_total), (2, 0, 1))
    out_list = result.reshape(KB, -1)
    lse_list = log_total.reshape(KB, -1)
    return (out_list, lse_list)


def general_body(
    queries,
    key_cache,
    value_cache,
    block_index,
    stream,
    out_weight,
    norm_gain,
    gate_weight,
    up_weight,
    down_weight,
):
    n_context = lax.axis_size("ctx")
    context_index = lax.axis_index("ctx")
    context_len = key_cache.shape[0] * n_context
    gathered = lax.all_gather(queries, "ctx", axis=0, tiled=True)
    part_out, part_lse = local_attention(
        gathered, key_cache, value_cache, block_index, context_index, context_len
    )
    spread_out, spread_lse = (
        lax.all_to_all(part_out[:, None, :], "ctx", split_axis=0, concat_axis=1, tiled=True),
        lax.all_to_all(part_lse[:, None, :], "ctx", split_axis=0, concat_axis=1, tiled=True),
    )
    share_rows = spread_out.shape[0]
    head_count = spread_lse.shape[2]
    peak_value = jnp.max(spread_lse, axis=1, keepdims=True)
    share_weight = jnp.exp(spread_lse - peak_value)
    blended = jnp.sum(
        spread_out.reshape(share_rows, n_context, head_count, -1) * share_weight[..., None], axis=1
    )
    blended = blended / jnp.sum(share_weight, axis=1)[..., None]
    attention = lax.all_gather(
        blended.reshape(share_rows, -1).astype(jnp.bfloat16), "ctx", axis=0, tiled=True
    )
    row_piece = attention
    projected = lax.psum_scatter(
        jnp.dot(row_piece, out_weight, preferred_element_type=jnp.float32),
        ("head", "sec"),
        scatter_dimension=0,
        tiled=True,
    )
    middle = (stream.astype(jnp.float32) + projected).astype(jnp.bfloat16)
    full_middle = lax.all_gather(middle, "ctx", axis=1, tiled=True)
    middle_wide = full_middle.astype(jnp.float32)
    mean_square = jnp.mean(middle_wide * middle_wide, axis=-1, keepdims=True)
    normed = (middle_wide * lax.rsqrt(mean_square + 1e-05) * norm_gain).astype(jnp.bfloat16)
    normed_cols, middle_cols = (
        lax.all_to_all(normed, ("head", "sec"), split_axis=1, concat_axis=0, tiled=True),
        lax.all_to_all(full_middle, ("head", "sec"), split_axis=1, concat_axis=0, tiled=True),
    )
    row_piece = normed_cols
    gate_up = lax.psum_scatter(
        jnp.concatenate(
            [
                jnp.dot(row_piece, gate_weight, preferred_element_type=jnp.float32),
                jnp.dot(row_piece, up_weight, preferred_element_type=jnp.float32),
            ],
            axis=1,
        ),
        ("head", "sec"),
        scatter_dimension=0,
        tiled=True,
    )
    hidden_width = gate_weight.shape[1]
    hidden = (jax.nn.silu(gate_up[:, :hidden_width]) * gate_up[:, hidden_width:]).astype(
        jnp.bfloat16
    )
    all_hidden = lax.all_gather(hidden, ("head", "sec"), axis=0, tiled=True)
    row_piece = all_hidden
    down_part = lax.psum_scatter(
        jnp.dot(row_piece, down_weight, preferred_element_type=jnp.float32),
        "ctx",
        scatter_dimension=0,
        tiled=True,
    )
    own_middle = lax.dynamic_slice_in_dim(
        middle_cols, context_index * down_part.shape[0], down_part.shape[0], 0
    )
    return (own_middle.astype(jnp.float32) + down_part).astype(jnp.bfloat16)


def solution(mesh):
    size = dict(mesh.shape)
    direct = size["ctx"] == 4 and size["head"] == 2 and size["sec"] == 2
    return jax.shard_map(
        direct_body if direct else general_body,
        mesh=mesh,
        in_specs=(
            P(("groups", "ctx"), ("head", "sec")),
            P(("groups", "ctx"), ("head", "sec")),
            P(("groups", "ctx"), ("head", "sec")),
            P("groups", None),
            P(("groups", "head", "sec"), "ctx"),
            P(("head", "sec"), "ctx"),
            P(),
            P(("head", "sec"), "ctx"),
            P(("head", "sec"), "ctx"),
            P("ctx", ("head", "sec")),
        ),
        out_specs=P(("groups", "ctx"), ("head", "sec")),
        check_vma=False,
    )
```

profile of v0, /device:TPU:0, one launch (start us, length us, event | category | flops | bytes accessed | tf_op | source)
XLA Modules:
  0.0 118.8 jit_solution(18206421861492607459)
XLA Ops:
  0.0 3.1 %collective-permute-start = (bf16[32,2048]{1,0:T(8,128)(2,1)}, bf16[32,2048]{1,0:T(8,128)(2,1)S(1)}, u32[]{:S(2)}, u32[]{:S(2)}) collective-permute-start(bf16[32,2048]{1,0:T(8,128)(2,1)} %q_ref.1), channel_id=1, source_target_pairs={{0,4},{4,0},{8,12},{12,8},{1,5},{5,1},{9,13},{13,9},{2,6},{6,2},{1... | collective-permute-start | bytes 393224 | tf_op jit(solution)/shard_map/ppermute | solution.py:307
  3.1 2.6 %collective-permute-start.2 = (bf16[32,2048]{1,0:T(8,128)(2,1)}, bf16[32,2048]{1,0:T(8,128)(2,1)S(1)}, u32[]{:S(2)}, u32[]{:S(2)}) collective-permute-start(bf16[32,2048]{1,0:T(8,128)(2,1)} %q_ref.1), channel_id=1, source_target_pairs={{0,8},{4,12},{8,0},{12,4},{1,9},{5,13},{9,1},{13,5},{2,10},{6,14},... | collective-permute-start | bytes 393224 | tf_op jit(solution)/shard_map/ppermute | solution.py:307
  5.7 0.7 copy-done.3
  6.4 1.7 %shard_map.100 = (bf16[512,256]{1,0:T(8,128)(2,1)S(1)}, bf16[512,256]{1,0:T(8,128)(2,1)S(1)}) custom-call(s32[1,8]{1,0:T(1,128)S(1)} %copy-done.3, s32[4]{0:T(128)S(1)} %pad_add_fusion.meta_ref, bf16[2048,256]{1,0:T(8,128)(2,1)} %key_ref.1, bf16[2048,256]{1,0:T(8,128)(2,1)} %value_ref.1), custom_call_target="tpu_custom_call" | custom-call | flops 3000000000 | bytes 2621488 | tf_op jit(solution)/shard_map/pallas_call | solution.py:37
  8.3 1.4 %shard_map.102 = bf16[32,2176]{1,0:T(8,128)(2,1)S(1)} custom-call(s32[1,8]{1,0:T(1,128)S(1)} %copy-done.3, s32[4]{0:T(128)S(1)} %pad_add_fusion.meta_ref, bf16[32,2048]{1,0:T(8,128)(2,1)S(1)} %collective-permute-done.q_ref, bf16[512,256]{1,0:T(8,128)(2,1)S(1)} %get-tuple-element.25.key_ref, bf16[512,256]{1,0:T(8,128)(2,1)S(1)} %get-tuple-element.26.value_ref), custom_call_target="tpu_custom_call" | custom-call | flops 3000000000 | bytes 794672 | tf_op jit(solution)/shard_map/pallas_call | solution.py:37
  9.7 0.7 collective-permute-start.1
  10.4 5.8 %collective-permute-done.2.q_ref = bf16[32,2048]{1,0:T(8,128)(2,1)S(1)} collective-permute-done((bf16[32,2048]{1,0:T(8,128)(2,1)}, bf16[32,2048]{1,0:T(8,128)(2,1)S(1)}, u32[]{:S(2)}, u32[]{:S(2)}) %collective-permute-start.2) | collective-permute-done | bytes 131104 | tf_op jit(solution)/shard_map/ppermute | solution.py:307
  16.1 1.4 %shard_map.103 = bf16[32,2176]{1,0:T(8,128)(2,1)S(1)} custom-call(s32[1,8]{1,0:T(1,128)S(1)} %copy-done.3, s32[4]{0:T(128)S(1)} %pad_add_fusion.meta_ref, bf16[32,2048]{1,0:T(8,128)(2,1)S(1)} %collective-permute-done.2.q_ref, bf16[512,256]{1,0:T(8,128)(2,1)S(1)} %get-tuple-element.25.key_ref, bf16[512,256]{1,0:T(8,128)(2,1)S(1)} %get-tuple-element.26.value_ref), custom_call_target="tpu_custom_call" | custom-call | flops 3000000000 | bytes 794672 | tf_op jit(solution)/shard_map/pallas_call | solution.py:37
  17.6 1.4 %shard_map.104 = bf16[32,2176]{1,0:T(8,128)(2,1)S(1)} custom-call(s32[1,8]{1,0:T(1,128)S(1)} %copy-done.3, s32[4]{0:T(128)S(1)} %pad_add_fusion.meta_ref, bf16[32,2048]{1,0:T(8,128)(2,1)S(1)} %collective-permute-done.4.q_ref, bf16[512,256]{1,0:T(8,128)(2,1)S(1)} %get-tuple-element.25.key_ref, bf16[512,256]{1,0:T(8,128)(2,1)S(1)} %get-tuple-element.26.value_ref), custom_call_target="tpu_custom_call" | custom-call | flops 3000000000 | bytes 794672 | tf_op jit(solution)/shard_map/pallas_call | solution.py:37
  19.0 2.3 %collective-permute-start.5 = (bf16[32,2176]{1,0:T(8,128)(2,1)S(1)}, bf16[32,2176]{1,0:T(8,128)(2,1)S(1)}, u32[]{:S(2)}, u32[]{:S(2)}) collective-permute-start(bf16[32,2176]{1,0:T(8,128)(2,1)S(1)} %shard_map.104), channel_id=1, source_target_pairs={{0,12},{4,8},{8,4},{12,0},{1,13},{5,9},{9,5},{13,1},{2,14},{6,10},... | collective-permute-start | bytes 417800 | tf_op jit(solution)/shard_map/ppermute | solution.py:307
  21.3 1.4 %shard_map.101.refs_0_ = bf16[32,2176]{1,0:T(8,128)(2,1)S(1)} custom-call(s32[1,8]{1,0:T(1,128)S(1)} %copy-done.3, s32[4]{0:T(128)S(1)} %pad_add_fusion.meta_ref, bf16[32,2048]{1,0:T(8,128)(2,1)S(1)} %copy-done.1, bf16[512,256]{1,0:T(8,128)(2,1)S(1)} %get-tuple-element.25.key_ref, bf16[512,256]{1,0:T(8,128)(2,1)S(1)} %get-tuple-element.26.value_ref), custom_call_target="tpu_custom_call" | custom-call | flops 3000000000 | bytes 794672 | tf_op jit(solution)/shard_map/pallas_call | solution.py:37
  22.7 5.2 %collective-permute-done.3.refs_2_ = bf16[32,2176]{1,0:T(8,128)(2,1)S(1)} collective-permute-done((bf16[32,2176]{1,0:T(8,128)(2,1)S(1)}, bf16[32,2176]{1,0:T(8,128)(2,1)S(1)}, u32[]{:S(2)}, u32[]{:S(2)}) %collective-permute-start.3) | collective-permute-done | bytes 139296 | tf_op jit(solution)/shard_map/ppermute | solution.py:307
  28.4 2.6 %collective-permute-start.6 = (bf16[32,2048]{1,0:T(8,128)(2,1)S(1)}, bf16[32,2048]{1,0:T(8,128)(2,1)S(1)}, u32[]{:S(2)}, u32[]{:S(2)}) collective-permute-start(bf16[32,2048]{1,0:T(8,128)(2,1)S(1)} %shard_map.105.refs_0_), channel_id=1, source_target_pairs={{0,4},{4,0},{8,12},{12,8},{1,5},{5,1},{9,13},{13,9},{2,6},{6,2},{1... | collective-permute-start | bytes 393224 | tf_op jit(solution)/shard_map/ppermute | solution.py:307
  31.0 0.7 collective-permute-start.7
  31.7 1.7 %collective-permute-start.8 = (bf16[32,2048]{1,0:T(8,128)(2,1)S(1)}, bf16[32,2048]{1,0:T(8,128)(2,1)S(1)}, u32[]{:S(2)}, u32[]{:S(2)}) collective-permute-start(bf16[32,2048]{1,0:T(8,128)(2,1)S(1)} %shard_map.105.refs_0_), channel_id=1, source_target_pairs={{0,12},{4,8},{8,4},{12,0},{1,13},{5,9},{9,5},{13,1},{2,14},{6,10},... | collective-permute-start | bytes 393224 | tf_op jit(solution)/shard_map/ppermute | solution.py:307
  33.5 1.5 %collective-permute-done.6.refs_1_ = bf16[32,2048]{1,0:T(8,128)(2,1)S(1)} collective-permute-done((bf16[32,2048]{1,0:T(8,128)(2,1)S(1)}, bf16[32,2048]{1,0:T(8,128)(2,1)S(1)}, u32[]{:S(2)}, u32[]{:S(2)}) %collective-permute-start.6) | collective-permute-done | bytes 131104 | tf_op jit(solution)/shard_map/ppermute | solution.py:307
  35.0 7.4 %collective-permute-done.7.refs_2_ = bf16[32,2048]{1,0:T(8,128)(2,1)S(1)} collective-permute-done((bf16[32,2048]{1,0:T(8,128)(2,1)S(1)}, bf16[32,2048]{1,0:T(8,128)(2,1)S(1)}, u32[]{:S(2)}, u32[]{:S(2)}) %collective-permute-start.7) | collective-permute-done | bytes 131104 | tf_op jit(solution)/shard_map/ppermute | solution.py:307
  42.4 1.9 %shard_map.106 = (f32[64,2048]{1,0:T(8,128)S(1)}, bf16[64,2048]{1,0:T(8,128)(2,1)S(1)}) custom-call(s32[4]{0:T(128)S(1)} %pad_add_fusion.meta_ref, bf16[32,2048]{1,0:T(8,128)(2,1)S(1)} %shard_map.105.refs_0_, bf16[32,2048]{1,0:T(8,128)(2,1)S(1)} %collective-permute-done.6.refs_1_, bf16[32,2048]{1,0:T(8,128)(2,1)S(1)} %collective-permute-done.7.refs_2_, ...), custom_call_target="tpu_custom_call" | custom-call | flops 3000000000 | bytes 9699344 | tf_op jit(solution)/shard_map/pallas_call | solution.py:37
  44.4 1.5 %collective-permute-done.9.got_ref = bf16[64,2048]{1,0:T(8,128)(2,1)S(1)} collective-permute-done((bf16[64,2048]{1,0:T(8,128)(2,1)S(1)}, bf16[64,2048]{1,0:T(8,128)(2,1)S(1)}, u32[]{:S(2)}, u32[]{:S(2)}) %collective-permute-start.9) | collective-permute-done | bytes 262176 | tf_op jit(solution)/shard_map/ppermute | solution.py:303
  45.9 0.6 shard_map.107
  46.5 1.5 %collective-permute-start.10 = (bf16[32,2048]{1,0:T(8,128)(2,1)S(1)}, bf16[32,2048]{1,0:T(8,128)(2,1)S(1)}, u32[]{:S(2)}, u32[]{:S(2)}) collective-permute-start(bf16[32,2048]{1,0:T(8,128)(2,1)S(1)} %get-tuple-element.30), channel_id=1, source_target_pairs={{0,2},{2,0},{1,3},{3,1},{4,6},{6,4},{5,7},{7,5},{8,10},{10,8},{9,1... | collective-permute-start | bytes 393224 | tf_op jit(solution)/shard_map/ppermute | solution.py:303
  48.1 4.1 %collective-permute-done.10.got_ref = bf16[32,2048]{1,0:T(8,128)(2,1)S(1)} collective-permute-done((bf16[32,2048]{1,0:T(8,128)(2,1)S(1)}, bf16[32,2048]{1,0:T(8,128)(2,1)S(1)}, u32[]{:S(2)}, u32[]{:S(2)}) %collective-permute-start.10) | collective-permute-done | bytes 131104 | tf_op jit(solution)/shard_map/ppermute | solution.py:303
  52.2 0.8 collective-permute-start.11
  53.0 3.5 %collective-permute-start.12 = (bf16[32,2048]{1,0:T(8,128)(2,1)S(1)}, bf16[32,2048]{1,0:T(8,128)(2,1)S(1)}, u32[]{:S(2)}, u32[]{:S(2)}) collective-permute-start(bf16[32,2048]{1,0:T(8,128)(2,1)S(1)} %shard_map.108), channel_id=1, source_target_pairs={{0,4},{1,0},{2,12},{3,8},{4,5},{5,1},{6,13},{7,9},{8,6},{9,2},{10,... | collective-permute-start | bytes 393224 | tf_op jit(solution)/shard_map/ppermute | solution.py:380
  56.5 2.8 %collective-permute-start.13 = (bf16[32,2048]{1,0:T(8,128)(2,1)S(1)}, bf16[32,2048]{1,0:T(8,128)(2,1)S(1)}, u32[]{:S(2)}, u32[]{:S(2)}) collective-permute-start(bf16[32,2048]{1,0:T(8,128)(2,1)S(1)} %shard_map.108), channel_id=1, source_target_pairs={{0,8},{1,12},{2,0},{3,4},{4,9},{5,13},{6,1},{7,5},{8,10},{9,14},{1... | collective-permute-start | bytes 393224 | tf_op jit(solution)/shard_map/ppermute | solution.py:380
  59.3 0.7 collective-permute-done.12.refs_1_
  60.0 6.4 %collective-permute-done.13.refs_2_ = bf16[32,2048]{1,0:T(8,128)(2,1)S(1)} collective-permute-done((bf16[32,2048]{1,0:T(8,128)(2,1)S(1)}, bf16[32,2048]{1,0:T(8,128)(2,1)S(1)}, u32[]{:S(2)}, u32[]{:S(2)}) %collective-permute-start.13) | collective-permute-done | bytes 131104 | tf_op jit(solution)/shard_map/ppermute | solution.py:380
  66.8 3.0 %shard_map.109 = (f32[64,2944]{1,0:T(8,128)S(1)}, bf16[64,3072]{1,0:T(8,128)(2,1)S(1)}) custom-call(s32[4]{0:T(128)S(1)} %pad_add_fusion.meta_ref, bf16[32,2048]{1,0:T(8,128)(2,1)S(1)} %collective-permute-done.11.refs_0_.middle_ref, bf16[32,2048]{1,0:T(8,128)(2,1)S(1)} %collective-permute-done.12.refs_1_, ...), custom_call_target="tpu_custom_call" | custom-call | flops 3000000000 | bytes 31064080 | tf_op jit(solution)/shard_map/pallas_call | solution.py:37
  69.9 3.3 %shard_map.112 = (f32[64,4352]{1,0:T(8,128)S(1)}, bf16[64,4352]{1,0:T(8,128)(2,1)S(1)}) custom-call(s32[4]{0:T(128)S(1)} %pad_add_fusion.meta_ref, bf16[32,2048]{1,0:T(8,128)(2,1)S(1)} %collective-permute-done.11.refs_0_.middle_ref, bf16[32,2048]{1,0:T(8,128)(2,1)S(1)} %collective-permute-done.12.refs_1_, ...), custom_call_target="tpu_custom_call" | custom-call | flops 3000000000 | bytes 31588368 | tf_op jit(solution)/shard_map/pallas_call | solution.py:37
  73.2 0.6 collective-permute-start.17
  73.8 0.6 shard_map.110
  74.4 6.4 %collective-permute-start.16 = (bf16[32,3072]{1,0:T(8,128)(2,1)S(1)}, bf16[32,3072]{1,0:T(8,128)(2,1)S(1)}, u32[]{:S(2)}, u32[]{:S(2)}) collective-permute-start(bf16[32,3072]{1,0:T(8,128)(2,1)S(1)} %get-tuple-element.34), channel_id=1, source_target_pairs={{0,2},{2,0},{1,3},{3,1},{4,6},{6,4},{5,7},{7,5},{8,10},{10,8},{9,1... | collective-permute-start | bytes 589832 | tf_op jit(solution)/shard_map/ppermute | solution.py:303
  80.8 0.7 shard_map.113
  81.5 1.0 collective-permute-start.18
  82.5 4.1 %collective-permute-done.16.got_ref = bf16[32,3072]{1,0:T(8,128)(2,1)S(1)} collective-permute-done((bf16[32,3072]{1,0:T(8,128)(2,1)S(1)}, bf16[32,3072]{1,0:T(8,128)(2,1)S(1)}, u32[]{:S(2)}, u32[]{:S(2)}) %collective-permute-start.16) | collective-permute-done | bytes 196640 | tf_op jit(solution)/shard_map/ppermute | solution.py:303
  86.7 5.2 %collective-permute-done.18.got_ref = bf16[32,4352]{1,0:T(8,128)(2,1)S(1)} collective-permute-done((bf16[32,4352]{1,0:T(8,128)(2,1)S(1)}, bf16[32,4352]{1,0:T(8,128)(2,1)S(1)}, u32[]{:S(2)}, u32[]{:S(2)}) %collective-permute-start.18) | collective-permute-done | bytes 278560 | tf_op jit(solution)/shard_map/ppermute | solution.py:303
  92.0 1.8 %collective-permute-start.22 = (bf16[32,2176]{1,0:T(8,128)(2,1)S(1)}, bf16[32,2176]{1,0:T(8,128)(2,1)S(1)}, u32[]{:S(2)}, u32[]{:S(2)}) collective-permute-start(bf16[32,2176]{1,0:T(8,128)(2,1)S(1)} %shard_map.114.refs_1_), channel_id=1, source_target_pairs={{0,2},{2,0},{1,3},{3,1},{4,6},{6,4},{5,7},{7,5},{8,10},{10,8},{9,1... | collective-permute-start | bytes 417800 | tf_op jit(solution)/shard_map/ppermute | solution.py:303
  94.1 4.0 %collective-permute-done.22.refs_5_ = bf16[32,2176]{1,0:T(8,128)(2,1)S(1)} collective-permute-done((bf16[32,2176]{1,0:T(8,128)(2,1)S(1)}, bf16[32,2176]{1,0:T(8,128)(2,1)S(1)}, u32[]{:S(2)}, u32[]{:S(2)}) %collective-permute-start.22) | collective-permute-done | bytes 139296 | tf_op jit(solution)/shard_map/ppermute | solution.py:303
  98.1 0.5 collective-permute-start.19
  99.0 0.5 collective-permute-done.19.refs_2_
  99.6 0.8 collective-permute-done.23.refs_6_
  100.4 2.7 %shard_map.115 = (f32[32,2048]{1,0:T(8,128)S(1)}, bf16[32,2048]{1,0:T(8,128)(2,1)S(1)}, bf16[32,2048]{1,0:T(8,128)(2,1)S(1)}, bf16[32,2048]{1,0:T(8,128)(2,1)S(1)}) custom-call(s32[4]{0:T(128)S(1)} %pad_add_fusion.meta_ref, bf16[32,1408]{1,0:T(8,128)(2,1)S(1)} %get-tuple-element.35.refs_0_, bf16[32,2176]{1,0:T(8,128)(2,1)S(1)} %shard_map.114.refs_1_, ...), custom_call_target="tpu_custom_call" | custom-call | flops 3000000000 | bytes 16252944 | tf_op jit(solution)/shard_map/pallas_call | solution.py:37
  103.1 3.8 %collective-permute-start.25 = (bf16[32,2048]{1,0:T(8,128)(2,1)S(1)}, bf16[32,2048]{1,0:T(8,128)(2,1)S(1)}, u32[]{:S(2)}, u32[]{:S(2)}) collective-permute-start(bf16[32,2048]{1,0:T(8,128)(2,1)S(1)} %get-tuple-element.42), channel_id=1, source_target_pairs={{0,12},{4,8},{8,4},{12,0},{1,13},{5,9},{9,5},{13,1},{2,14},{6,10},... | collective-permute-start | bytes 393224 | tf_op jit(solution)/shard_map/ppermute | solution.py:307
  106.9 0.6 collective-permute-start.27
  107.6 3.8 %collective-permute-done.25.refs_0_ = bf16[32,2048]{1,0:T(8,128)(2,1)S(1)} collective-permute-done((bf16[32,2048]{1,0:T(8,128)(2,1)S(1)}, bf16[32,2048]{1,0:T(8,128)(2,1)S(1)}, u32[]{:S(2)}, u32[]{:S(2)}) %collective-permute-start.25) | collective-permute-done | bytes 131104 | tf_op jit(solution)/shard_map/ppermute | solution.py:307
  111.4 3.5 %collective-permute-done.26.refs_1_ = bf16[32,2048]{1,0:T(8,128)(2,1)S(1)} collective-permute-done((bf16[32,2048]{1,0:T(8,128)(2,1)S(1)}, bf16[32,2048]{1,0:T(8,128)(2,1)S(1)}, u32[]{:S(2)}, u32[]{:S(2)}) %collective-permute-start.26) | collective-permute-done | bytes 131104 | tf_op jit(solution)/shard_map/ppermute | solution.py:307
  114.9 3.2 %collective-permute-done.27.refs_2_ = bf16[32,2048]{1,0:T(8,128)(2,1)S(1)} collective-permute-done((bf16[32,2048]{1,0:T(8,128)(2,1)S(1)}, bf16[32,2048]{1,0:T(8,128)(2,1)S(1)}, u32[]{:S(2)}, u32[]{:S(2)}) %collective-permute-start.27) | collective-permute-done | bytes 131104 | tf_op jit(solution)/shard_map/ppermute | solution.py:307
  118.1 0.7 shard_map.116
  (66 shorter events, 2.5 us)
Async XLA Ops:
  0.0 8.3 %collective-permute-start = (bf16[32,2048]{1,0:T(8,128)(2,1)}, bf16[32,2048]{1,0:T(8,128)(2,1)S(1)}, u32[]{:S(2)}, u32[]{:S(2)}) collective-permute-start(bf16[32,2048]{1,0:T(8,128)(2,1)} %q_ref.1), channel_id=1, source_target_pairs={{0,4},{4,0},{8,12},{12,8},{1,5},{5,1},{9,13},{13,9},{2,6},{6,2},{1... | collective-permute-start | bytes 393224 | tf_op jit(solution)/shard_map/ppermute | solution.py:307
  3.1 13.1 %collective-permute-start.2 = (bf16[32,2048]{1,0:T(8,128)(2,1)}, bf16[32,2048]{1,0:T(8,128)(2,1)S(1)}, u32[]{:S(2)}, u32[]{:S(2)}) collective-permute-start(bf16[32,2048]{1,0:T(8,128)(2,1)} %q_ref.1), channel_id=1, source_target_pairs={{0,8},{4,12},{8,0},{12,4},{1,9},{5,13},{9,1},{13,5},{2,10},{6,14},... | collective-permute-start | bytes 393224 | tf_op jit(solution)/shard_map/ppermute | solution.py:307
  5.6 11.9 %collective-permute-start.4 = (bf16[32,2048]{1,0:T(8,128)(2,1)}, bf16[32,2048]{1,0:T(8,128)(2,1)S(1)}, u32[]{:S(2)}, u32[]{:S(2)}) collective-permute-start(bf16[32,2048]{1,0:T(8,128)(2,1)} %q_ref.1), channel_id=1, source_target_pairs={{0,12},{4,8},{8,4},{12,0},{1,13},{5,9},{9,5},{13,1},{2,14},{6,10},... | collective-permute-start | bytes 393224 | tf_op jit(solution)/shard_map/ppermute | solution.py:307
  5.7 0.7 copy-start.3
  8.3 13.0 %copy-start.1 = (bf16[32,2048]{1,0:T(8,128)(2,1)S(1)}, bf16[32,2048]{1,0:T(8,128)(2,1)}, u32[]{:S(2)}) copy-start(bf16[32,2048]{1,0:T(8,128)(2,1)} %q_ref.1) | copy-start | bytes 393220
  9.7 13.0 %collective-permute-start.1 = (bf16[32,2176]{1,0:T(8,128)(2,1)S(1)}, bf16[32,2176]{1,0:T(8,128)(2,1)S(1)}, u32[]{:S(2)}, u32[]{:S(2)}) collective-permute-start(bf16[32,2176]{1,0:T(8,128)(2,1)S(1)} %shard_map.102), channel_id=1, source_target_pairs={{0,4},{4,0},{8,12},{12,8},{1,5},{5,1},{9,13},{13,9},{2,6},{6,2},{1... | collective-permute-start | bytes 417800 | tf_op jit(solution)/shard_map/ppermute | solution.py:307
  17.5 24.9 %slice-start.12 = ((s8[8388608]{0:T(1024)(128)(4,1)}), s8[4194304]{0:T(1024)(128)(4,1)S(1)}, s32[]{:S(2)}) async-start(s8[8388608]{0:T(1024)(128)(4,1)} %bitcast.13), calls=%async_computation.12 | async-start | bytes 8388608
  17.5 10.4 %collective-permute-start.3 = (bf16[32,2176]{1,0:T(8,128)(2,1)S(1)}, bf16[32,2176]{1,0:T(8,128)(2,1)S(1)}, u32[]{:S(2)}, u32[]{:S(2)}) collective-permute-start(bf16[32,2176]{1,0:T(8,128)(2,1)S(1)} %shard_map.103), channel_id=1, source_target_pairs={{0,8},{4,12},{8,0},{12,4},{1,9},{5,13},{9,1},{13,5},{2,10},{6,14},... | collective-permute-start | bytes 417800 | tf_op jit(solution)/shard_map/ppermute | solution.py:307
  19.0 23.5 %slice-start.13 = ((s8[8388608]{0:T(1024)(128)(4,1)}), s8[4194304]{0:T(1024)(128)(4,1)S(1)}, s32[]{:S(2)}) async-start(s8[8388608]{0:T(1024)(128)(4,1)} %bitcast.13), calls=%async_computation.13 | async-start | bytes 8388608
  19.0 9.0 %collective-permute-start.5 = (bf16[32,2176]{1,0:T(8,128)(2,1)S(1)}, bf16[32,2176]{1,0:T(8,128)(2,1)S(1)}, u32[]{:S(2)}, u32[]{:S(2)}) collective-permute-start(bf16[32,2176]{1,0:T(8,128)(2,1)S(1)} %shard_map.104), channel_id=1, source_target_pairs={{0,12},{4,8},{8,4},{12,0},{1,13},{5,9},{9,5},{13,1},{2,14},{6,10},... | collective-permute-start | bytes 417800 | tf_op jit(solution)/shard_map/ppermute | solution.py:307
  28.4 23.8 %copy-start.2 = (bf16[32,2048]{1,0:T(8,128)(2,1)S(1)}, bf16[32,2048]{1,0:T(8,128)(2,1)}, u32[]{:S(2)}) copy-start(bf16[32,2048]{1,0:T(8,128)(2,1)} %stream_ref.1) | copy-start | bytes 393220
  28.4 6.6 %collective-permute-start.6 = (bf16[32,2048]{1,0:T(8,128)(2,1)S(1)}, bf16[32,2048]{1,0:T(8,128)(2,1)S(1)}, u32[]{:S(2)}, u32[]{:S(2)}) collective-permute-start(bf16[32,2048]{1,0:T(8,128)(2,1)S(1)} %shard_map.105.refs_0_), channel_id=1, source_target_pairs={{0,4},{4,0},{8,12},{12,8},{1,5},{5,1},{9,13},{13,9},{2,6},{6,2},{1... | collective-permute-start | bytes 393224 | tf_op jit(solution)/shard_map/ppermute | solution.py:307
  31.0 11.4 %collective-permute-start.7 = (bf16[32,2048]{1,0:T(8,128)(2,1)S(1)}, bf16[32,2048]{1,0:T(8,128)(2,1)S(1)}, u32[]{:S(2)}, u32[]{:S(2)}) collective-permute-start(bf16[32,2048]{1,0:T(8,128)(2,1)S(1)} %shard_map.105.refs_0_), channel_id=1, source_target_pairs={{0,8},{4,12},{8,0},{12,4},{1,9},{5,13},{9,1},{13,5},{2,10},{6,14},... | collective-permute-start | bytes 393224 | tf_op jit(solution)/shard_map/ppermute | solution.py:307
  31.7 10.7 %collective-permute-start.8 = (bf16[32,2048]{1,0:T(8,128)(2,1)S(1)}, bf16[32,2048]{1,0:T(8,128)(2,1)S(1)}, u32[]{:S(2)}, u32[]{:S(2)}) collective-permute-start(bf16[32,2048]{1,0:T(8,128)(2,1)S(1)} %shard_map.105.refs_0_), channel_id=1, source_target_pairs={{0,12},{4,8},{8,4},{12,0},{1,13},{5,9},{9,5},{13,1},{2,14},{6,10},... | collective-permute-start | bytes 393224 | tf_op jit(solution)/shard_map/ppermute | solution.py:307
  44.3 1.6 %collective-permute-start.9 = (bf16[64,2048]{1,0:T(8,128)(2,1)S(1)}, bf16[64,2048]{1,0:T(8,128)(2,1)S(1)}, u32[]{:S(2)}, u32[]{:S(2)}) collective-permute-start(bf16[64,2048]{1,0:T(8,128)(2,1)S(1)} %get-tuple-element.28), channel_id=1, source_target_pairs={{0,1},{1,0},{2,3},{3,2},{4,5},{5,4},{6,7},{7,6},{8,9},{9,8},{10,11... | collective-permute-start | bytes 786440 | tf_op jit(solution)/shard_map/ppermute | solution.py:303
  45.9 20.8 %slice-start = ((s8[14680064]{0:T(1024)(128)(4,1)}), s8[4194304]{0:T(1024)(128)(4,1)S(1)}, s32[]{:S(2)}) async-start(s8[14680064]{0:T(1024)(128)(4,1)} %bitcast.5), calls=%async_computation | async-start | bytes 8388608
  45.9 20.8 %slice-start.1 = ((s8[14680064]{0:T(1024)(128)(4,1)}), s8[4194304]{0:T(1024)(128)(4,1)S(1)}, s32[]{:S(2)}) async-start(s8[14680064]{0:T(1024)(128)(4,1)} %bitcast.5), calls=%async_computation.1 | async-start | bytes 8388608
  45.9 20.8 %slice-start.4 = ((s8[14680064]{0:T(1024)(128)(4,1)}), s8[2097152]{0:T(1024)(128)(4,1)S(1)}, s32[]{:S(2)}) async-start(s8[14680064]{0:T(1024)(128)(4,1)} %bitcast.7), calls=%async_computation.4 | async-start | bytes 4194304
  45.9 20.8 %slice-start.5 = ((s8[14680064]{0:T(1024)(128)(4,1)}), s8[4194304]{0:T(1024)(128)(4,1)S(1)}, s32[]{:S(2)}) async-start(s8[14680064]{0:T(1024)(128)(4,1)} %bitcast.7), calls=%async_computation.5 | async-start | bytes 8388608
  46.5 20.2 %copy-start = (f32[8192]{0:T(1024)S(1)}, f32[8192]{0:T(1024)}, u32[]{:S(2)}) copy-start(f32[8192]{0:T(1024)} %param.16) | copy-start | bytes 98308
  46.5 20.2 %slice-start.2 = ((s8[14680064]{0:T(1024)(128)(4,1)}), s8[4194304]{0:T(1024)(128)(4,1)S(1)}, s32[]{:S(2)}) async-start(s8[14680064]{0:T(1024)(128)(4,1)} %bitcast.5), calls=%async_computation.2 | async-start | bytes 8388608
  46.5 20.2 %slice-start.6 = ((s8[14680064]{0:T(1024)(128)(4,1)}), s8[4194304]{0:T(1024)(128)(4,1)S(1)}, s32[]{:S(2)}) async-start(s8[14680064]{0:T(1024)(128)(4,1)} %bitcast.7), calls=%async_computation.6 | async-start | bytes 8388608
  46.5 5.6 %collective-permute-start.10 = (bf16[32,2048]{1,0:T(8,128)(2,1)S(1)}, bf16[32,2048]{1,0:T(8,128)(2,1)S(1)}, u32[]{:S(2)}, u32[]{:S(2)}) collective-permute-start(bf16[32,2048]{1,0:T(8,128)(2,1)S(1)} %get-tuple-element.30), channel_id=1, source_target_pairs={{0,2},{2,0},{1,3},{3,1},{4,6},{6,4},{5,7},{7,5},{8,10},{10,8},{9,1... | collective-permute-start | bytes 393224 | tf_op jit(solution)/shard_map/ppermute | solution.py:303
  52.1 14.6 %slice-start.3 = ((s8[14680064]{0:T(1024)(128)(4,1)}), s8[2097152]{0:T(1024)(128)(4,1)S(1)}, s32[]{:S(2)}) async-start(s8[14680064]{0:T(1024)(128)(4,1)} %bitcast.5), calls=%async_computation.3 | async-start | bytes 4194304
  52.2 14.6 %slice-start.7 = ((s8[14680064]{0:T(1024)(128)(4,1)}), s8[4194304]{0:T(1024)(128)(4,1)S(1)}, s32[]{:S(2)}) async-start(s8[14680064]{0:T(1024)(128)(4,1)} %bitcast.7), calls=%async_computation.7 | async-start | bytes 8388608
  52.2 7.1 %collective-permute-start.11 = (bf16[32,2048]{1,0:T(8,128)(2,1)S(1)}, bf16[32,2048]{1,0:T(8,128)(2,1)S(1)}, u32[]{:S(2)}, u32[]{:S(2)}) collective-permute-start(bf16[32,2048]{1,0:T(8,128)(2,1)S(1)} %shard_map.108), channel_id=1, source_target_pairs={{0,0},{1,4},{2,8},{3,12},{4,1},{5,5},{6,9},{7,13},{8,2},{9,6},{10,... | collective-permute-start | bytes 393224 | tf_op jit(solution)/shard_map/ppermute | solution.py:380
  53.0 7.0 %collective-permute-start.12 = (bf16[32,2048]{1,0:T(8,128)(2,1)S(1)}, bf16[32,2048]{1,0:T(8,128)(2,1)S(1)}, u32[]{:S(2)}, u32[]{:S(2)}) collective-permute-start(bf16[32,2048]{1,0:T(8,128)(2,1)S(1)} %shard_map.108), channel_id=1, source_target_pairs={{0,4},{1,0},{2,12},{3,8},{4,5},{5,1},{6,13},{7,9},{8,6},{9,2},{10,... | collective-permute-start | bytes 393224 | tf_op jit(solution)/shard_map/ppermute | solution.py:380
  56.5 9.9 %collective-permute-start.13 = (bf16[32,2048]{1,0:T(8,128)(2,1)S(1)}, bf16[32,2048]{1,0:T(8,128)(2,1)S(1)}, u32[]{:S(2)}, u32[]{:S(2)}) collective-permute-start(bf16[32,2048]{1,0:T(8,128)(2,1)S(1)} %shard_map.108), channel_id=1, source_target_pairs={{0,8},{1,12},{2,0},{3,4},{4,9},{5,13},{6,1},{7,5},{8,10},{9,14},{1... | collective-permute-start | bytes 393224 | tf_op jit(solution)/shard_map/ppermute | solution.py:380
  59.3 7.4 %collective-permute-start.14 = (bf16[32,2048]{1,0:T(8,128)(2,1)S(1)}, bf16[32,2048]{1,0:T(8,128)(2,1)S(1)}, u32[]{:S(2)}, u32[]{:S(2)}) collective-permute-start(bf16[32,2048]{1,0:T(8,128)(2,1)S(1)} %shard_map.108), channel_id=1, source_target_pairs={{0,12},{1,8},{2,4},{3,0},{4,13},{5,9},{6,5},{7,1},{8,14},{9,10},{1... | collective-permute-start | bytes 393224 | tf_op jit(solution)/shard_map/ppermute | solution.py:380
  69.8 4.0 %collective-permute-start.15 = (bf16[64,3072]{1,0:T(8,128)(2,1)S(1)}, bf16[64,3072]{1,0:T(8,128)(2,1)S(1)}, u32[]{:S(2)}, u32[]{:S(2)}) collective-permute-start(bf16[64,3072]{1,0:T(8,128)(2,1)S(1)} %get-tuple-element.32), channel_id=1, source_target_pairs={{0,1},{1,0},{2,3},{3,2},{4,5},{5,4},{6,7},{7,6},{8,9},{9,8},{10,11... | collective-permute-start | bytes 1179656 | tf_op jit(solution)/shard_map/ppermute | solution.py:303
  73.2 7.6 %collective-permute-start.17 = (bf16[64,4352]{1,0:T(8,128)(2,1)S(1)}, bf16[64,4352]{1,0:T(8,128)(2,1)S(1)}, u32[]{:S(2)}, u32[]{:S(2)}) collective-permute-start(bf16[64,4352]{1,0:T(8,128)(2,1)S(1)} %get-tuple-element.38), channel_id=1, source_target_pairs={{0,1},{1,0},{2,3},{3,2},{4,5},{5,4},{6,7},{7,6},{8,9},{9,8},{10,11... | collective-permute-start | bytes 1671176 | tf_op jit(solution)/shard_map/ppermute | solution.py:303
  74.4 12.1 %collective-permute-start.16 = (bf16[32,3072]{1,0:T(8,128)(2,1)S(1)}, bf16[32,3072]{1,0:T(8,128)(2,1)S(1)}, u32[]{:S(2)}, u32[]{:S(2)}) collective-permute-start(bf16[32,3072]{1,0:T(8,128)(2,1)S(1)} %get-tuple-element.34), channel_id=1, source_target_pairs={{0,2},{2,0},{1,3},{3,1},{4,6},{6,4},{5,7},{7,5},{8,10},{10,8},{9,1... | collective-permute-start | bytes 589832 | tf_op jit(solution)/shard_map/ppermute | solution.py:303
  80.8 19.5 %slice-start.8 = ((s8[14680064]{0:T(1024)(128)(4,1)}), s8[4194304]{0:T(1024)(128)(4,1)S(1)}, s32[]{:S(2)}) async-start(s8[14680064]{0:T(1024)(128)(4,1)} %bitcast.9), calls=%async_computation.8 | async-start | bytes 8388608
  80.8 19.5 %slice-start.9 = ((s8[14680064]{0:T(1024)(128)(4,1)}), s8[4194304]{0:T(1024)(128)(4,1)S(1)}, s32[]{:S(2)}) async-start(s8[14680064]{0:T(1024)(128)(4,1)} %bitcast.9), calls=%async_computation.9 | async-start | bytes 8388608
  81.5 10.4 %collective-permute-start.18 = (bf16[32,4352]{1,0:T(8,128)(2,1)S(1)}, bf16[32,4352]{1,0:T(8,128)(2,1)S(1)}, u32[]{:S(2)}, u32[]{:S(2)}) collective-permute-start(bf16[32,4352]{1,0:T(8,128)(2,1)S(1)} %get-tuple-element.40), channel_id=1, source_target_pairs={{0,2},{2,0},{1,3},{3,1},{4,6},{6,4},{5,7},{7,5},{8,10},{10,8},{9,1... | collective-permute-start | bytes 835592 | tf_op jit(solution)/shard_map/ppermute | solution.py:303
  86.6 13.8 %slice-start.10 = ((s8[14680064]{0:T(1024)(128)(4,1)}), s8[4194304]{0:T(1024)(128)(4,1)S(1)}, s32[]{:S(2)}) async-start(s8[14680064]{0:T(1024)(128)(4,1)} %bitcast.9), calls=%async_computation.10 | async-start | bytes 8388608
  91.9 8.5 %slice-start.11 = ((s8[14680064]{0:T(1024)(128)(4,1)}), s8[2097152]{0:T(1024)(128)(4,1)S(1)}, s32[]{:S(2)}) async-start(s8[14680064]{0:T(1024)(128)(4,1)} %bitcast.9), calls=%async_computation.11 | async-start | bytes 4194304
  92.0 6.1 %collective-permute-start.22 = (bf16[32,2176]{1,0:T(8,128)(2,1)S(1)}, bf16[32,2176]{1,0:T(8,128)(2,1)S(1)}, u32[]{:S(2)}, u32[]{:S(2)}) collective-permute-start(bf16[32,2176]{1,0:T(8,128)(2,1)S(1)} %shard_map.114.refs_1_), channel_id=1, source_target_pairs={{0,2},{2,0},{1,3},{3,1},{4,6},{6,4},{5,7},{7,5},{8,10},{10,8},{9,1... | collective-permute-start | bytes 417800 | tf_op jit(solution)/shard_map/ppermute | solution.py:303
  93.8 5.2 %collective-permute-start.21 = (bf16[32,1408]{1,0:T(8,128)(2,1)S(1)}, bf16[32,1408]{1,0:T(8,128)(2,1)S(1)}, u32[]{:S(2)}, u32[]{:S(2)}) collective-permute-start(bf16[32,1408]{1,0:T(8,128)(2,1)S(1)} %get-tuple-element.35.refs_0_), channel_id=1, source_target_pairs={{0,2},{2,0},{1,3},{3,1},{4,6},{6,4},{5,7},{7,5},{8,10},{10,8},{9,1... | collective-permute-start | bytes 270344 | tf_op jit(solution)/shard_map/ppermute | solution.py:303
  94.1 6.2 %collective-permute-start.20 = (bf16[32,2176]{1,0:T(8,128)(2,1)S(1)}, bf16[32,2176]{1,0:T(8,128)(2,1)S(1)}, u32[]{:S(2)}, u32[]{:S(2)}) collective-permute-start(bf16[32,2176]{1,0:T(8,128)(2,1)S(1)} %shard_map.114.refs_1_), channel_id=1, source_target_pairs={{0,1},{1,0},{2,3},{3,2},{4,5},{5,4},{6,7},{7,6},{8,9},{9,8},{10,11... | collective-permute-start | bytes 417800 | tf_op jit(solution)/shard_map/ppermute | solution.py:303
  98.1 2.3 %collective-permute-start.24 = (bf16[32,2176]{1,0:T(8,128)(2,1)S(1)}, bf16[32,2176]{1,0:T(8,128)(2,1)S(1)}, u32[]{:S(2)}, u32[]{:S(2)}) collective-permute-start(bf16[32,2176]{1,0:T(8,128)(2,1)S(1)} %collective-permute-done.22.refs_5_), channel_id=1, source_target_pairs={{0,1},{1,0},{2,3},{3,2},{4,5},{5,4},{6,7},{7,6},{8,9},{9,8},{10,11... | collective-permute-start | bytes 417800 | tf_op jit(solution)/shard_map/ppermute | solution.py:303
  98.1 1.5 %collective-permute-start.19 = (bf16[32,1408]{1,0:T(8,128)(2,1)S(1)}, bf16[32,1408]{1,0:T(8,128)(2,1)S(1)}, u32[]{:S(2)}, u32[]{:S(2)}) collective-permute-start(bf16[32,1408]{1,0:T(8,128)(2,1)S(1)} %get-tuple-element.35.refs_0_), channel_id=1, source_target_pairs={{0,1},{1,0},{2,3},{3,2},{4,5},{5,4},{6,7},{7,6},{8,9},{9,8},{10,11... | collective-permute-start | bytes 270344 | tf_op jit(solution)/shard_map/ppermute | solution.py:303
  99.0 1.3 %collective-permute-start.23 = (bf16[32,1408]{1,0:T(8,128)(2,1)S(1)}, bf16[32,1408]{1,0:T(8,128)(2,1)S(1)}, u32[]{:S(2)}, u32[]{:S(2)}) collective-permute-start(bf16[32,1408]{1,0:T(8,128)(2,1)S(1)} %collective-permute-done.21.refs_4_), channel_id=1, source_target_pairs={{0,1},{1,0},{2,3},{3,2},{4,5},{5,4},{6,7},{7,6},{8,9},{9,8},{10,11... | collective-permute-start | bytes 270344 | tf_op jit(solution)/shard_map/ppermute | solution.py:303
  103.1 8.3 %collective-permute-start.25 = (bf16[32,2048]{1,0:T(8,128)(2,1)S(1)}, bf16[32,2048]{1,0:T(8,128)(2,1)S(1)}, u32[]{:S(2)}, u32[]{:S(2)}) collective-permute-start(bf16[32,2048]{1,0:T(8,128)(2,1)S(1)} %get-tuple-element.42), channel_id=1, source_target_pairs={{0,12},{4,8},{8,4},{12,0},{1,13},{5,9},{9,5},{13,1},{2,14},{6,10},... | collective-permute-start | bytes 393224 | tf_op jit(solution)/shard_map/ppermute | solution.py:307
  106.9 7.9 %collective-permute-start.26 = (bf16[32,2048]{1,0:T(8,128)(2,1)S(1)}, bf16[32,2048]{1,0:T(8,128)(2,1)S(1)}, u32[]{:S(2)}, u32[]{:S(2)}) collective-permute-start(bf16[32,2048]{1,0:T(8,128)(2,1)S(1)} %get-tuple-element.43), channel_id=1, source_target_pairs={{0,4},{4,0},{8,12},{12,8},{1,5},{5,1},{9,13},{13,9},{2,6},{6,2},{1... | collective-permute-start | bytes 393224 | tf_op jit(solution)/shard_map/ppermute | solution.py:307
  106.9 11.2 %collective-permute-start.27 = (bf16[32,2048]{1,0:T(8,128)(2,1)S(1)}, bf16[32,2048]{1,0:T(8,128)(2,1)S(1)}, u32[]{:S(2)}, u32[]{:S(2)}) collective-permute-start(bf16[32,2048]{1,0:T(8,128)(2,1)S(1)} %get-tuple-element.44), channel_id=1, source_target_pairs={{0,8},{4,12},{8,0},{12,4},{1,9},{5,13},{9,1},{13,5},{2,10},{6,14},... | collective-permute-start | bytes 393224 | tf_op jit(solution)/shard_map/ppermute | solution.py:307
where the time goes:
time: 119 us
  waiting for transfers between devices  58.7 us (49%)
  starting transfers between devices  37.6 us (32%)
  Pallas kernels  21.5 us (18%)
    ppermute x12, waiting for transfers between devices, turn(): return lax.ppermute(x, axis, [(i, i ^ offset) for i in range(n)])  30.7 us
    pallas_call x17, Pallas kernels, call(): pl.pallas_call(kernel, out_shape=out, in_specs=in_specs, out_specs=jax.tr...  21.5 us
    ppermute x12, waiting for transfers between devices, swap(): return lax.ppermute(x, axis, [(0, 1), (1, 0)])  20.6 us
    ppermute x12, starting transfers between devices, turn(): return lax.ppermute(x, axis, [(i, i ^ offset) for i in range(n)])  18.3 us
    ppermute x12, starting transfers between devices, swap(): return lax.ppermute(x, axis, [(0, 1), (1, 0)])  12.2 us
    ppermute x4, waiting for transfers between devices, direct_body(): lax.ppermute(middle, ALL, [(a * n_context + b, (b ^ m) * n_context + a) f...  7.38 us
    ppermute x4, starting transfers between devices, direct_body(): lax.ppermute(middle, ALL, [(a * n_context + b, (b ^ m) * n_context + a) f...  7.09 us
  transfers between devices with their start and end apart: 28, of which 19 were waited for; matrix products, arithmetic and copies ran while one was open for 0% of the time, Pallas kernels for 10%

commit v1 on v0

--- a/solution.py
+++ b/solution.py
@@ -53,93 +53,106 @@
     return pltpu.with_memory_space_constraint(x, pltpu.HBM)
 
 
-def slots(index_ref, shard, blocks):
+N_META = 4
+
+
+def slots(meta_ref, blocks):
+    entries = meta_ref.shape[0] - N_META
+    base = meta_ref[0] * blocks
     first = jnp.int32(0)
-    count = jnp.int32(0)
-    for n in range(index_ref.shape[1]):
-        block = index_ref[0, n]
-        first += (block < shard * blocks).astype(jnp.int32)
-        count += (block < (shard + 1) * blocks).astype(jnp.int32)
-    return first, count - first
-
-
-def slot_block(index_ref, first, count, slot, shard, blocks):
-    entry = jnp.minimum(first + slot, index_ref.shape[1] - 1)
-    local = jnp.clip(index_ref[0, entry] - shard * blocks, 0, blocks - 1)
-    return local, slot < count
-
-
-def pick_kernel(index_ref, meta_ref, key_ref, value_ref, key_out, value_out, sems):
-    blocks = key_ref.shape[0] // KB
-    shard = meta_ref[0]
-    first, count = slots(index_ref, shard, blocks)
-    copies = []
+    end = jnp.int32(0)
+    for n in range(entries):
+        block = meta_ref[N_META + n]
+        first += (block < base).astype(jnp.int32)
+        end += (block < base + blocks).astype(jnp.int32)
+    found = []
     for slot in range(MOST):
-        local, _ = slot_block(index_ref, first, count, slot, shard, blocks)
-        rows = pl.ds(pl.multiple_of(local * KB, KB), KB)
-        for n, (src, dst) in enumerate(((key_ref, key_out), (value_ref, value_out))):
-            copy = pltpu.make_async_copy(
-                src.at[rows, :], dst.at[slot * KB : (slot + 1) * KB, :], sems.at[n, slot]
-            )
-            copy.start()
-            copies.append(copy)
-    for copy in copies:
-        copy.wait()
-
-
-def attend_kernel(offset, blocks, context_len, total, index_ref, meta_ref, q_ref, key_ref, value_ref, out_ref):
+        entry = jnp.minimum(first + slot, entries - 1)
+        local = jnp.clip(meta_ref[N_META + entry] - base, 0, blocks - 1)
+        found.append((local, first + slot < end))
+    return found
+
+
+def attend(offset, blocks, context_len, total, meta_ref, q_ref, key_ref, value_ref, out_ref, score_ref, weight_ref):
     rows = q_ref.shape[0]
     heads = q_ref.shape[1] // DH
     kv_dev = key_ref.shape[1] // DH
     group = heads // kv_dev
     shard = meta_ref[0]
+    scale = 1.0 / math.sqrt(DH)
     token0 = context_len - total + (shard ^ offset) * rows
-    first, count = slots(index_ref, shard, blocks)
-    limits = []
-    for slot in range(MOST):
-        local, valid = slot_block(index_ref, first, count, slot, shard, blocks)
-        limit = token0 - (shard * blocks + local) * KB
-        limits.append(jnp.where(valid, limit, jnp.int32(-(1 << 20))))
-    row = lax.broadcasted_iota(jnp.int32, (group * rows, KB), 0) % rows
-    lane = lax.broadcasted_iota(jnp.int32, (group * rows, KB), 1)
-    ahead = lane - row
+    limits = [
+        jnp.where(valid, token0 - (shard * blocks + local) * KB, jnp.int32(-(1 << 20)))
+        for local, valid in slots(meta_ref, blocks)
+    ]
+    ahead = lax.broadcasted_iota(jnp.int32, (rows, KB), 1) - lax.broadcasted_iota(
+        jnp.int32, (rows, KB), 0
+    )
+    allowed = [ahead <= limit for limit in limits]
     head_lane = lax.broadcasted_iota(jnp.int32, (rows, LANES), 1)
     lse_tile = jnp.zeros((rows, LANES), F32)
     for kv in range(kv_dev):
         stacked = jnp.concatenate(
             [q_ref[:, (kv * group + h) * DH : (kv * group + h + 1) * DH] for h in range(group)], axis=0
         )
-        scores = lax.dot_general(
+        score_ref[kv] = lax.dot_general(
             stacked,
             key_ref[:, kv * DH : (kv + 1) * DH],
             (((1,), (1,)), ((), ())),
             preferred_element_type=F32,
-        ) * (1.0 / math.sqrt(DH))
-        parts = [
-            jnp.where(ahead <= limits[slot], scores[:, slot * KB : (slot + 1) * KB], -1e30)
-            for slot in range(MOST)
-        ]
-        peak = functools.reduce(jnp.maximum, parts)
-        peak = jnp.max(peak, axis=1, keepdims=True)
-        parts = [jnp.exp(p - peak) for p in parts]
-        row_total = jnp.sum(functools.reduce(jnp.add, parts), axis=1, keepdims=True)
-        weights = jnp.concatenate([p.astype(BF16) for p in parts], axis=1)
-        mixture = jnp.dot(
-            weights, value_ref[:, kv * DH : (kv + 1) * DH], preferred_element_type=F32
-        )
-        mixture = (mixture * (1.0 / row_total)).astype(BF16)
-        lse = peak + jnp.log(row_total)
+        )
+    for kv in range(kv_dev):
+        totals = []
         for h in range(group):
             head = kv * group + h
             span = slice(h * rows, (h + 1) * rows)
-            out_ref[:, head * DH : (head + 1) * DH] = mixture[span]
-            lse_tile = jnp.where(head_lane == head, lse[span], lse_tile)
+            parts = [
+                jnp.where(allowed[slot], score_ref[kv, span, slot * KB : (slot + 1) * KB], -1e30)
+                for slot in range(MOST)
+            ]
+            peak = jnp.max(functools.reduce(jnp.maximum, parts), axis=1, keepdims=True)
+            parts = [jnp.exp((p - peak) * scale) for p in parts]
+            row_total = jnp.sum(functools.reduce(jnp.add, parts), axis=1, keepdims=True)
+            for slot, p in enumerate(parts):
+                weight_ref[kv, span, slot * KB : (slot + 1) * KB] = p.astype(BF16)
+            totals.append(1.0 / row_total)
+            lse_tile = jnp.where(head_lane == head, peak * scale + jnp.log(row_total), lse_tile)
+        mixture = jnp.dot(
+            weight_ref[kv], value_ref[:, kv * DH : (kv + 1) * DH], preferred_element_type=F32
+        )
+        for h in range(group):
+            head = kv * group + h
+            out_ref[:, head * DH : (head + 1) * DH] = (
+                mixture[h * rows : (h + 1) * rows] * totals[h]
+            ).astype(BF16)
     high = lse_tile.astype(BF16).astype(F32)
     rest = lse_tile - high
     mid = rest.astype(BF16).astype(F32)
     low = rest - mid
     tile = high + pltpu.roll(mid, heads, 1) + pltpu.roll(low, 2 * heads, 1)
     out_ref[:, heads * DH :] = tile.astype(BF16)
+
+
+def first_attend_kernel(
+    blocks, context_len, total, meta_ref, q_hbm, key_hbm, value_hbm,
+    key_ref, value_ref, out_ref, q_ref, score_ref, weight_ref, sems, q_sem,
+):
+    copies = [pltpu.make_async_copy(q_hbm, q_ref, q_sem)]
+    for slot, (local, _) in enumerate(slots(meta_ref, blocks)):
+        rows = pl.ds(pl.multiple_of(local * KB, KB), KB)
+        for n, (src, dst) in enumerate(((key_hbm, key_ref), (value_hbm, value_ref))):
+            copies.append(
+                pltpu.make_async_copy(
+                    src.at[rows, :], dst.at[slot * KB : (slot + 1) * KB, :], sems.at[n, slot]
+                )
+            )
+    for copy in copies:
+        copy.start()
+    for copy in copies:
+        copy.wait()
+    attend(
+        0, blocks, context_len, total, meta_ref, q_ref, key_ref, value_ref, out_ref, score_ref, weight_ref
+    )
 
 
 def blend_kernel(*refs):
@@ -218,28 +231,36 @@
     return tile[:, :LANES].astype(F32) + tile[:, LANES:].astype(F32)
 
 
-def gate_kernel(n_sec, start, width, tile, with_norm, meta_ref, *refs):
-    pieces = refs[:4]
-    gain_ref, gate_ref, up_ref, keep_ref, send_ref, rows_ref = refs[4:]
+def prepare_kernel(meta_ref, piece_ref, gain_ref, row_ref, square_ref):
+    model = piece_ref.shape[1]
+    gain = gain_ref[:, pl.ds(pl.multiple_of(meta_ref[3] * model, model), model)]
+    wide = piece_ref[...].astype(F32)
+    row_ref[...] = (wide * gain).astype(BF16)
+    square_ref[...] = jnp.broadcast_to(jnp.sum(wide * wide, axis=1, keepdims=True), square_ref.shape)
+
+
+def first_gate_kernel(n_sec, width, tile, meta_ref, *refs):
+    pieces, squares = refs[:4], refs[4:8]
+    gate_ref, up_ref, keep_ref, send_ref, rows_ref = refs[8:]
     rows = pieces[0].shape[0]
     half = rows_ref.shape[0] // 2
-    model = rows_ref.shape[1]
-    gain = gain_ref[:, pl.ds(pl.multiple_of(meta_ref[3] * model, model), model)]
-    for n, piece in enumerate(pieces):
-        wide = piece[...].astype(F32)
+    for n, (piece, square) in enumerate(zip(pieces, squares)):
         at = place_of(meta_ref, n_sec, n, rows, len(pieces))
-        rows_ref[pl.ds(at, rows), :] = (wide * gain).astype(BF16)
-        if with_norm:
-            square = jnp.broadcast_to(jnp.sum(wide * wide, axis=1, keepdims=True), (rows, LANES))
-
-            @pl.when(at < half)
-            def _():
-                keep_ref[pl.ds(at, rows), 2 * width :] = square
-
-            @pl.when(at >= half)
-            def _():
-                put_exact(send_ref, pl.ds(pl.multiple_of(at - half, rows), rows), 2 * width, square)
-
+        rows_ref[pl.ds(at, rows), :] = piece[...]
+
+        @pl.when(at < half)
+        def _():
+            keep_ref[pl.ds(at, rows), 2 * width :] = square[...]
+
+        @pl.when(at >= half)
+        def _():
+            put_exact(send_ref, pl.ds(pl.multiple_of(at - half, rows), rows), 2 * width, square[...])
+
+    product(rows_ref, gate_ref, 0, keep_ref, send_ref, 0, width, tile)
+    product(rows_ref, up_ref, 0, keep_ref, send_ref, width, width, tile)
+
+
+def gate_kernel(start, width, tile, rows_ref, gate_ref, up_ref, keep_ref, send_ref):
     product(rows_ref, gate_ref, start, keep_ref, send_ref, 0, width, tile)
     product(rows_ref, up_ref, start, keep_ref, send_ref, width, width, tile)
 
@@ -322,7 +343,9 @@
     n_context, n_head, n_sec = (lax.axis_size(a) for a in ALL)
     shard, head, sec = (lax.axis_index(a) for a in ALL)
     place = head * n_sec + sec
-    meta = jnp.stack([shard, head, sec, place]).astype(jnp.int32)
+    meta = jnp.concatenate(
+        [jnp.stack([shard, head, sec, place]).astype(jnp.int32), block_index[0]]
+    )
     rows, heads_width = queries.shape
     context_len = key_cache.shape[0] * n_context
     model = norm_gain.shape[0]
@@ -332,22 +355,31 @@
     order = (3, 1, 2)
 
     got_q = {m: turn(queries, "ctx", n_context, m) for m in order}
-    got_q[0] = queries
     picked = struct((MOST * KB, kv_width), BF16)
-    keys, values = call(
-        pick_kernel,
-        (picked, picked),
-        [SM, SM, ANY, ANY],
-        (block_index, meta, in_hbm(key_cache), in_hbm(value_cache)),
-        scratch=[pltpu.SemaphoreType.DMA((2, MOST))],
-    )
-    partial = {}
-    for m in (0,) + order:
+    partial_out = struct((rows, heads_width + LANES), BF16)
+    kv_dev = kv_width // DH
+    tall = heads_width // kv_width * rows
+    scratch = [
+        pltpu.VMEM((kv_dev, tall, MOST * KB), F32),
+        pltpu.VMEM((kv_dev, tall, MOST * KB), BF16),
+    ]
+    keys, values, own_partial = call(
+        functools.partial(first_attend_kernel, blocks, context_len, total),
+        (picked, picked, partial_out),
+        [SM, ANY, ANY, ANY],
+        (meta, in_hbm(queries), in_hbm(key_cache), in_hbm(value_cache)),
+        scratch=[pltpu.VMEM((rows, heads_width), BF16)]
+        + scratch
+        + [pltpu.SemaphoreType.DMA((2, MOST)), pltpu.SemaphoreType.DMA],
+    )
+    partial = {0: own_partial}
+    for m in order:
         partial[m] = call(
-            functools.partial(attend_kernel, m, blocks, context_len, total),
-            struct((rows, heads_width + LANES), BF16),
-            [SM, SM, VM, VM, VM],
-            (block_index, meta, got_q[m], keys, values),
+            functools.partial(attend, m, blocks, context_len, total),
+            partial_out,
+            [SM, VM, VM, VM],
+            (meta, got_q[m], keys, values),
+            scratch=scratch,
         )
     back = {m: turn(partial[m], "ctx", n_context, m) for m in order}
     back[0] = partial[0]
@@ -389,24 +421,43 @@
         for m in (3, 0, 1, 2)
     }
     hidden_width = gate_weight.shape[1]
-    units = hidden_width // LANES
-    first = units * 2 // 5 * LANES
+    first = hidden_width // 2 // LANES * LANES
     chunks = ((0, first), (first, hidden_width - first))
     hidden = []
     gate_vmem, up_vmem = in_vmem(gate_weight), in_vmem(up_weight)
+    prepared = [
+        call(
+            prepare_kernel,
+            (struct((rows, width), BF16), struct((rows, LANES), F32)),
+            [SM, VM, VM],
+            (meta, all_middle[m], norm_gain[None]),
+        )
+        for m in range(4)
+    ]
     scale = None
     for c, (start, chunk) in enumerate(chunks):
         extra = LANES if c == 0 else 0
-        keep, away = call(
-            functools.partial(gate_kernel, n_sec, start, chunk, 256, c == 0),
-            (
-                struct((n_head * rows, 2 * chunk + extra), F32),
-                struct((n_head * rows, 2 * chunk + 2 * extra), BF16),
-            ),
-            [SM] + [VM] * 7,
-            (meta,) + tuple(all_middle[m] for m in range(4)) + (norm_gain[None], gate_vmem, up_vmem),
-            scratch=[pltpu.VMEM((total, width), BF16)],
-        )
+        out = (
+            struct((n_head * rows, 2 * chunk + extra), F32),
+            struct((n_head * rows, 2 * chunk + 2 * extra), BF16),
+        )
+        if c == 0:
+            keep, away, all_rows = call(
+                functools.partial(first_gate_kernel, n_sec, chunk, 512),
+                out + (struct((total, width), BF16),),
+                [SM] + [VM] * 10,
+                (meta,)
+                + tuple(p[0] for p in prepared)
+                + tuple(p[1] for p in prepared)
+                + (gate_vmem, up_vmem),
+            )
+        else:
+            keep, away = call(
+                functools.partial(gate_kernel, start, chunk, 512),
+                out,
+                [VM] * 3,
+                (all_rows, gate_vmem, up_vmem),
+            )
         keep, away = call(
             functools.partial(fold_kernel, 2 * chunk),
             (

time: 119 us -> 119 us (level)
  local copies, waits for them, and re-layouts: 0.73 us -> 6.61 us
  waiting for transfers between devices: 58.7 us -> 54.6 us
  starting transfers between devices: 37.6 us -> 35.4 us
    unnamed x36 -> x32, local copies, waits for them, and re-layouts: 0.73 us -> 5.88 us
    ppermute x4, starting transfers between devices: 7.09 us -> 3.55 us  [direct_body(): lax.ppermute(middle, ALL, [(a * n_context + b, (b ^ m) * n_context + a) f...]
    ppermute x12, waiting for transfers between devices: 20.6 us -> 17.2 us  [swap(): return lax.ppermute(x, axis, [(0, 1), (1, 0)])]
    ppermute x4, waiting for transfers between devices: 7.38 us -> 4.76 us  [direct_body(): lax.ppermute(middle, ALL, [(a * n_context + b, (b ^ m) * n_context + a) f...]
    ppermute x12, waiting for transfers between devices: 30.7 us -> 32.6 us  [turn(): return lax.ppermute(x, axis, [(i, i ^ offset) for i in range(n)])]
    pallas_call x17 -> x20, Pallas kernels: 21.5 us -> 21.9 us  [call(): pl.pallas_call(kernel, out_shape=out, in_specs=in_specs, out_specs=jax.tr...]
  transfers between devices with their start and end apart: 28 -> 28, of which waited for: 19 -> 14; matrix products, arithmetic and copies ran while one was open for 0% -> 1% of each run, Pallas kernels for 10% -> 10%
where the time goes in v1:
time: 119 us
  waiting for transfers between devices  54.6 us (46%)
  starting transfers between devices  35.4 us (30%)
  Pallas kernels  21.9 us (18%)
  local copies, waits for them, and re-layouts  6.61 us (6%)
    ppermute x12, waiting for transfers between devices, turn(): return lax.ppermute(x, axis, [(i, i ^ offset) for i in range(n)])  32.6 us
    pallas_call x20, Pallas kernels, call(): pl.pallas_call(kernel, out_shape=out, in_specs=in_specs, out_specs=jax.tr...  21.9 us
    ppermute x12, starting transfers between devices, turn(): return lax.ppermute(x, axis, [(i, i ^ offset) for i in range(n)])  19.5 us
    ppermute x12, waiting for transfers between devices, swap(): return lax.ppermute(x, axis, [(0, 1), (1, 0)])  17.2 us
    ppermute x12, starting transfers between devices, swap(): return lax.ppermute(x, axis, [(0, 1), (1, 0)])  12.3 us
    unnamed x32, local copies, waits for them, and re-layouts  5.88 us
    ppermute x4, waiting for transfers between devices, direct_body(): lax.ppermute(middle, ALL, [(a * n_context + b, (b ^ m) * n_context + a) f...  4.76 us
    ppermute x4, starting transfers between devices, direct_body(): lax.ppermute(middle, ALL, [(a * n_context + b, (b ^ m) * n_context + a) f...  3.55 us
  transfers between devices with their start and end apart: 28, of which 14 were waited for; matrix products, arithmetic and copies ran while one was open for 1% of the time, Pallas kernels for 10%

profile of v1, /device:TPU:0, one launch (start us, length us, event | category | flops | bytes accessed | tf_op | source)
XLA Modules:
  0.0 118.7 jit_solution(5753144696068694933)
XLA Ops:
  0.0 3.1 %collective-permute-start = (bf16[32,2048]{1,0:T(8,128)(2,1)}, bf16[32,2048]{1,0:T(8,128)(2,1)S(1)}, u32[]{:S(2)}, u32[]{:S(2)}) collective-permute-start(bf16[32,2048]{1,0:T(8,128)(2,1)} %q_hbm.1), channel_id=1, source_target_pairs={{0,4},{4,0},{8,12},{12,8},{1,5},{5,1},{9,13},{13,9},{2,6},{6,2},{1... | collective-permute-start | bytes 393224 | tf_op jit(solution)/shard_map/ppermute | solution.py:328
  3.1 2.5 %collective-permute-start.4 = (bf16[32,2048]{1,0:T(8,128)(2,1)}, bf16[32,2048]{1,0:T(8,128)(2,1)S(1)}, u32[]{:S(2)}, u32[]{:S(2)}) collective-permute-start(bf16[32,2048]{1,0:T(8,128)(2,1)} %q_hbm.1), channel_id=1, source_target_pairs={{0,12},{4,8},{8,4},{12,0},{1,13},{5,9},{9,5},{13,1},{2,14},{6,10},... | collective-permute-start | bytes 393224 | tf_op jit(solution)/shard_map/ppermute | solution.py:328
  5.6 0.7 concatenate.3.meta_ref
  6.4 2.5 %shard_map.100 = (bf16[512,256]{1,0:T(8,128)(2,1)S(1)}, bf16[512,256]{1,0:T(8,128)(2,1)S(1)}, bf16[32,2176]{1,0:T(8,128)(2,1)S(1)}) custom-call(s32[12]{0:T(128)S(1)} %concatenate.3.meta_ref, bf16[32,2048]{1,0:T(8,128)(2,1)} %q_hbm.1, bf16[2048,256]{1,0:T(8,128)(2,1)} %key_hbm.1, bf16[2048,256]{1,0:T(8,128)(2,1)} %value_hbm.1), custom_call_target="tpu_custom_call" | custom-call | flops 3000000000 | bytes 2891824 | tf_op jit(solution)/shard_map/pallas_call | solution.py:37
  8.9 1.3 %shard_map.101 = bf16[32,2176]{1,0:T(8,128)(2,1)S(1)} custom-call(s32[12]{0:T(128)S(1)} %concatenate.3.meta_ref, bf16[32,2048]{1,0:T(8,128)(2,1)S(1)} %collective-permute-done.q_ref, bf16[512,256]{1,0:T(8,128)(2,1)S(1)} %get-tuple-element.36.key_ref, bf16[512,256]{1,0:T(8,128)(2,1)S(1)} %get-tuple-element.37.value_ref), custom_call_target="tpu_custom_call" | custom-call | flops 3000000000 | bytes 794672 | tf_op jit(solution)/shard_map/pallas_call | solution.py:37
  10.1 1.9 %collective-permute-start.1 = (bf16[32,2176]{1,0:T(8,128)(2,1)S(1)}, bf16[32,2176]{1,0:T(8,128)(2,1)S(1)}, u32[]{:S(2)}, u32[]{:S(2)}) collective-permute-start(bf16[32,2176]{1,0:T(8,128)(2,1)S(1)} %shard_map.101), channel_id=1, source_target_pairs={{0,4},{4,0},{8,12},{12,8},{1,5},{5,1},{9,13},{13,9},{2,6},{6,2},{1... | collective-permute-start | bytes 417800 | tf_op jit(solution)/shard_map/ppermute | solution.py:328
  12.0 5.6 %collective-permute-done.2.q_ref = bf16[32,2048]{1,0:T(8,128)(2,1)S(1)} collective-permute-done((bf16[32,2048]{1,0:T(8,128)(2,1)}, bf16[32,2048]{1,0:T(8,128)(2,1)S(1)}, u32[]{:S(2)}, u32[]{:S(2)}) %collective-permute-start.2) | collective-permute-done | bytes 131104 | tf_op jit(solution)/shard_map/ppermute | solution.py:328
  17.6 1.3 %shard_map.102 = bf16[32,2176]{1,0:T(8,128)(2,1)S(1)} custom-call(s32[12]{0:T(128)S(1)} %concatenate.3.meta_ref, bf16[32,2048]{1,0:T(8,128)(2,1)S(1)} %collective-permute-done.2.q_ref, bf16[512,256]{1,0:T(8,128)(2,1)S(1)} %get-tuple-element.36.key_ref, bf16[512,256]{1,0:T(8,128)(2,1)S(1)} %get-tuple-element.37.value_ref), custom_call_target="tpu_custom_call" | custom-call | flops 3000000000 | bytes 794672 | tf_op jit(solution)/shard_map/pallas_call | solution.py:37
  19.0 1.3 %shard_map.103 = bf16[32,2176]{1,0:T(8,128)(2,1)S(1)} custom-call(s32[12]{0:T(128)S(1)} %concatenate.3.meta_ref, bf16[32,2048]{1,0:T(8,128)(2,1)S(1)} %collective-permute-done.4.q_ref, bf16[512,256]{1,0:T(8,128)(2,1)S(1)} %get-tuple-element.36.key_ref, bf16[512,256]{1,0:T(8,128)(2,1)S(1)} %get-tuple-element.37.value_ref), custom_call_target="tpu_custom_call" | custom-call | flops 3000000000 | bytes 794672 | tf_op jit(solution)/shard_map/pallas_call | solution.py:37
  20.2 2.6 %collective-permute-start.5 = (bf16[32,2176]{1,0:T(8,128)(2,1)S(1)}, bf16[32,2176]{1,0:T(8,128)(2,1)S(1)}, u32[]{:S(2)}, u32[]{:S(2)}) collective-permute-start(bf16[32,2176]{1,0:T(8,128)(2,1)S(1)} %shard_map.103), channel_id=1, source_target_pairs={{0,12},{4,8},{8,4},{12,0},{1,13},{5,9},{9,5},{13,1},{2,14},{6,10},... | collective-permute-start | bytes 417800 | tf_op jit(solution)/shard_map/ppermute | solution.py:328
  22.9 7.7 %collective-permute-done.3.refs_2_ = bf16[32,2176]{1,0:T(8,128)(2,1)S(1)} collective-permute-done((bf16[32,2176]{1,0:T(8,128)(2,1)S(1)}, bf16[32,2176]{1,0:T(8,128)(2,1)S(1)}, u32[]{:S(2)}, u32[]{:S(2)}) %collective-permute-start.3) | collective-permute-done | bytes 139296 | tf_op jit(solution)/shard_map/ppermute | solution.py:328
  31.1 1.5 %collective-permute-start.8 = (bf16[32,2048]{1,0:T(8,128)(2,1)S(1)}, bf16[32,2048]{1,0:T(8,128)(2,1)S(1)}, u32[]{:S(2)}, u32[]{:S(2)}) collective-permute-start(bf16[32,2048]{1,0:T(8,128)(2,1)S(1)} %shard_map.104.refs_0_), channel_id=1, source_target_pairs={{0,12},{4,8},{8,4},{12,0},{1,13},{5,9},{9,5},{13,1},{2,14},{6,10},... | collective-permute-start | bytes 393224 | tf_op jit(solution)/shard_map/ppermute | solution.py:328
  32.6 3.3 %collective-permute-start.7 = (bf16[32,2048]{1,0:T(8,128)(2,1)S(1)}, bf16[32,2048]{1,0:T(8,128)(2,1)S(1)}, u32[]{:S(2)}, u32[]{:S(2)}) collective-permute-start(bf16[32,2048]{1,0:T(8,128)(2,1)S(1)} %shard_map.104.refs_0_), channel_id=1, source_target_pairs={{0,8},{4,12},{8,0},{12,4},{1,9},{5,13},{9,1},{13,5},{2,10},{6,14},... | collective-permute-start | bytes 393224 | tf_op jit(solution)/shard_map/ppermute | solution.py:328
  35.9 2.7 %collective-permute-done.8.refs_3_ = bf16[32,2048]{1,0:T(8,128)(2,1)S(1)} collective-permute-done((bf16[32,2048]{1,0:T(8,128)(2,1)S(1)}, bf16[32,2048]{1,0:T(8,128)(2,1)S(1)}, u32[]{:S(2)}, u32[]{:S(2)}) %collective-permute-start.8) | collective-permute-done | bytes 131104 | tf_op jit(solution)/shard_map/ppermute | solution.py:328
  38.6 7.7 %collective-permute-done.7.refs_2_ = bf16[32,2048]{1,0:T(8,128)(2,1)S(1)} collective-permute-done((bf16[32,2048]{1,0:T(8,128)(2,1)S(1)}, bf16[32,2048]{1,0:T(8,128)(2,1)S(1)}, u32[]{:S(2)}, u32[]{:S(2)}) %collective-permute-start.7) | collective-permute-done | bytes 131104 | tf_op jit(solution)/shard_map/ppermute | solution.py:328
  46.3 1.8 %shard_map.105 = (f32[64,2048]{1,0:T(8,128)S(1)}, bf16[64,2048]{1,0:T(8,128)(2,1)S(1)}) custom-call(s32[12]{0:T(128)S(1)} %concatenate.3.meta_ref, bf16[32,2048]{1,0:T(8,128)(2,1)S(1)} %shard_map.104.refs_0_, bf16[32,2048]{1,0:T(8,128)(2,1)S(1)} %collective-permute-done.6.refs_1_, bf16[32,2048]{1,0:T(8,128)(2,1)S(1)} %collective-permute-done.7.refs_2_, ...), custom_call_target="tpu_custom_call" | custom-call | flops 3000000000 | bytes 9699376 | tf_op jit(solution)/shard_map/pallas_call | solution.py:37
  48.2 1.5 %collective-permute-done.9.got_ref = bf16[64,2048]{1,0:T(8,128)(2,1)S(1)} collective-permute-done((bf16[64,2048]{1,0:T(8,128)(2,1)S(1)}, bf16[64,2048]{1,0:T(8,128)(2,1)S(1)}, u32[]{:S(2)}, u32[]{:S(2)}) %collective-permute-start.9) | collective-permute-done | bytes 262176 | tf_op jit(solution)/shard_map/ppermute | solution.py:324
  50.4 1.6 %collective-permute-start.10 = (bf16[32,2048]{1,0:T(8,128)(2,1)S(1)}, bf16[32,2048]{1,0:T(8,128)(2,1)S(1)}, u32[]{:S(2)}, u32[]{:S(2)}) collective-permute-start(bf16[32,2048]{1,0:T(8,128)(2,1)S(1)} %get-tuple-element.41), channel_id=1, source_target_pairs={{0,2},{2,0},{1,3},{3,1},{4,6},{6,4},{5,7},{7,5},{8,10},{10,8},{9,1... | collective-permute-start | bytes 393224 | tf_op jit(solution)/shard_map/ppermute | solution.py:324
  51.9 4.0 %collective-permute-done.10.got_ref = bf16[32,2048]{1,0:T(8,128)(2,1)S(1)} collective-permute-done((bf16[32,2048]{1,0:T(8,128)(2,1)S(1)}, bf16[32,2048]{1,0:T(8,128)(2,1)S(1)}, u32[]{:S(2)}, u32[]{:S(2)}) %collective-permute-start.10) | collective-permute-done | bytes 131104 | tf_op jit(solution)/shard_map/ppermute | solution.py:324
  56.0 1.4 %collective-permute-start.14 = (bf16[32,2048]{1,0:T(8,128)(2,1)S(1)}, bf16[32,2048]{1,0:T(8,128)(2,1)S(1)}, u32[]{:S(2)}, u32[]{:S(2)}) collective-permute-start(bf16[32,2048]{1,0:T(8,128)(2,1)S(1)} %shard_map.107), channel_id=1, source_target_pairs={{0,12},{1,8},{2,4},{3,0},{4,13},{5,9},{6,5},{7,1},{8,14},{9,10},{1... | collective-permute-start | bytes 393224 | tf_op jit(solution)/shard_map/ppermute | solution.py:412
  57.4 1.5 %collective-permute-start.13 = (bf16[32,2048]{1,0:T(8,128)(2,1)S(1)}, bf16[32,2048]{1,0:T(8,128)(2,1)S(1)}, u32[]{:S(2)}, u32[]{:S(2)}) collective-permute-start(bf16[32,2048]{1,0:T(8,128)(2,1)S(1)} %shard_map.107), channel_id=1, source_target_pairs={{0,8},{1,12},{2,0},{3,4},{4,9},{5,13},{6,1},{7,5},{8,10},{9,14},{1... | collective-permute-start | bytes 393224 | tf_op jit(solution)/shard_map/ppermute | solution.py:412
  58.9 0.7 collective-permute-start.11
  59.6 4.8 %collective-permute-done.14.piece_ref = bf16[32,2048]{1,0:T(8,128)(2,1)S(1)} collective-permute-done((bf16[32,2048]{1,0:T(8,128)(2,1)S(1)}, bf16[32,2048]{1,0:T(8,128)(2,1)S(1)}, u32[]{:S(2)}, u32[]{:S(2)}) %collective-permute-start.14) | collective-permute-done | bytes 131104 | tf_op jit(solution)/shard_map/ppermute | solution.py:412
  64.3 0.7 shard_map.111
  65.0 0.7 shard_map.110
  65.7 0.7 shard_map.109
  66.4 0.7 shard_map.108
  67.2 1.3 %slice-done.1 = s8[4194304]{0:T(1024)(128)(4,1)S(1)} async-done(((s8[14680064]{0:T(1024)(128)(4,1)}), s8[4194304]{0:T(1024)(128)(4,1)S(1)}, s32[]{:S(2)}) %slice-start.1) | async-done | bytes 4194328
  68.5 1.2 %slice-done.6 = s8[4194304]{0:T(1024)(128)(4,1)S(1)} async-done(((s8[14680064]{0:T(1024)(128)(4,1)}), s8[4194304]{0:T(1024)(128)(4,1)S(1)}, s32[]{:S(2)}) %slice-start.6) | async-done | bytes 4194328
  69.7 1.4 %slice-done.2 = s8[4194304]{0:T(1024)(128)(4,1)S(1)} async-done(((s8[14680064]{0:T(1024)(128)(4,1)}), s8[4194304]{0:T(1024)(128)(4,1)S(1)}, s32[]{:S(2)}) %slice-start.2) | async-done | bytes 4194328
  71.0 1.2 %slice-done.7 = s8[4194304]{0:T(1024)(128)(4,1)S(1)} async-done(((s8[14680064]{0:T(1024)(128)(4,1)}), s8[4194304]{0:T(1024)(128)(4,1)S(1)}, s32[]{:S(2)}) %slice-start.7) | async-done | bytes 4194328
  72.9 2.9 %shard_map.112 = (f32[64,3712]{1,0:T(8,128)S(1)}, bf16[64,3840]{1,0:T(8,128)(2,1)S(1)}, bf16[128,2048]{1,0:T(8,128)(2,1)S(1)}) custom-call(s32[12]{0:T(128)S(1)} %concatenate.3.meta_ref, bf16[32,2048]{1,0:T(8,128)(2,1)S(1)} %get-tuple-element.42.refs_0_, bf16[32,2048]{1,0:T(8,128)(2,1)S(1)} %get-tuple-element.43.refs_1_, ...), custom_call_target="tpu_custom_call" | custom-call | flops 3000000000 | bytes 31916080 | tf_op jit(solution)/shard_map/pallas_call | solution.py:37
  75.9 2.1 %shard_map.115 = (f32[64,3584]{1,0:T(8,128)S(1)}, bf16[64,3584]{1,0:T(8,128)(2,1)S(1)}) custom-call(bf16[128,2048]{1,0:T(8,128)(2,1)S(1)} %get-tuple-element.56.rows_ref, bf16[2048,3584]{1,0:T(8,128)(2,1)S(1)} %bitcast.7, bf16[2048,3584]{1,0:T(8,128)(2,1)S(1)} %bitcast.9), custom_call_target="tpu_custom_call" | custom-call | flops 3000000000 | bytes 31260672 | tf_op jit(solution)/shard_map/pallas_call | solution.py:37
  78.6 0.7 shard_map.113
  79.2 4.6 %collective-permute-start.16 = (bf16[32,3840]{1,0:T(8,128)(2,1)S(1)}, bf16[32,3840]{1,0:T(8,128)(2,1)S(1)}, u32[]{:S(2)}, u32[]{:S(2)}) collective-permute-start(bf16[32,3840]{1,0:T(8,128)(2,1)S(1)} %get-tuple-element.53), channel_id=1, source_target_pairs={{0,2},{2,0},{1,3},{3,1},{4,6},{6,4},{5,7},{7,5},{8,10},{10,8},{9,1... | collective-permute-start | bytes 737288 | tf_op jit(solution)/shard_map/ppermute | solution.py:324
  84.5 0.8 collective-permute-start.18
  85.3 5.4 %collective-permute-done.16.got_ref = bf16[32,3840]{1,0:T(8,128)(2,1)S(1)} collective-permute-done((bf16[32,3840]{1,0:T(8,128)(2,1)S(1)}, bf16[32,3840]{1,0:T(8,128)(2,1)S(1)}, u32[]{:S(2)}, u32[]{:S(2)}) %collective-permute-start.16) | collective-permute-done | bytes 245792 | tf_op jit(solution)/shard_map/ppermute | solution.py:324
  90.8 2.1 %collective-permute-start.21 = (bf16[32,1792]{1,0:T(8,128)(2,1)S(1)}, bf16[32,1792]{1,0:T(8,128)(2,1)S(1)}, u32[]{:S(2)}, u32[]{:S(2)}) collective-permute-start(bf16[32,1792]{1,0:T(8,128)(2,1)S(1)} %get-tuple-element.54.refs_0_), channel_id=1, source_target_pairs={{0,2},{2,0},{1,3},{3,1},{4,6},{6,4},{5,7},{7,5},{8,10},{10,8},{9,1... | collective-permute-start | bytes 344072 | tf_op jit(solution)/shard_map/ppermute | solution.py:324
  92.9 2.7 %collective-permute-done.18.got_ref = bf16[32,3584]{1,0:T(8,128)(2,1)S(1)} collective-permute-done((bf16[32,3584]{1,0:T(8,128)(2,1)S(1)}, bf16[32,3584]{1,0:T(8,128)(2,1)S(1)}, u32[]{:S(2)}, u32[]{:S(2)}) %collective-permute-start.18) | collective-permute-done | bytes 229408 | tf_op jit(solution)/shard_map/ppermute | solution.py:324
  95.7 2.1 %collective-permute-start.22 = (bf16[32,1792]{1,0:T(8,128)(2,1)S(1)}, bf16[32,1792]{1,0:T(8,128)(2,1)S(1)}, u32[]{:S(2)}, u32[]{:S(2)}) collective-permute-start(bf16[32,1792]{1,0:T(8,128)(2,1)S(1)} %shard_map.117.refs_1_), channel_id=1, source_target_pairs={{0,2},{2,0},{1,3},{3,1},{4,6},{6,4},{5,7},{7,5},{8,10},{10,8},{9,1... | collective-permute-start | bytes 344072 | tf_op jit(solution)/shard_map/ppermute | solution.py:324
  98.3 2.3 %collective-permute-done.22.refs_5_ = bf16[32,1792]{1,0:T(8,128)(2,1)S(1)} collective-permute-done((bf16[32,1792]{1,0:T(8,128)(2,1)S(1)}, bf16[32,1792]{1,0:T(8,128)(2,1)S(1)}, u32[]{:S(2)}, u32[]{:S(2)}) %collective-permute-start.22) | collective-permute-done | bytes 114720 | tf_op jit(solution)/shard_map/ppermute | solution.py:324
  100.6 1.3 %collective-permute-done.24.refs_7_ = bf16[32,1792]{1,0:T(8,128)(2,1)S(1)} collective-permute-done((bf16[32,1792]{1,0:T(8,128)(2,1)S(1)}, bf16[32,1792]{1,0:T(8,128)(2,1)S(1)}, u32[]{:S(2)}, u32[]{:S(2)}) %collective-permute-start.24) | collective-permute-done | bytes 114720 | tf_op jit(solution)/shard_map/ppermute | solution.py:324
  101.9 2.7 %shard_map.118 = (f32[32,2048]{1,0:T(8,128)S(1)}, bf16[32,2048]{1,0:T(8,128)(2,1)S(1)}, bf16[32,2048]{1,0:T(8,128)(2,1)S(1)}, bf16[32,2048]{1,0:T(8,128)(2,1)S(1)}) custom-call(s32[12]{0:T(128)S(1)} %concatenate.3.meta_ref, bf16[32,1792]{1,0:T(8,128)(2,1)S(1)} %get-tuple-element.54.refs_0_, bf16[32,1792]{1,0:T(8,128)(2,1)S(1)} %shard_map.117.refs_1_, ...), custom_call_target="tpu_custom_call" | custom-call | flops 3000000000 | bytes 16252976 | tf_op jit(solution)/shard_map/pallas_call | solution.py:37
  104.6 2.4 %collective-permute-start.25 = (bf16[32,2048]{1,0:T(8,128)(2,1)S(1)}, bf16[32,2048]{1,0:T(8,128)(2,1)S(1)}, u32[]{:S(2)}, u32[]{:S(2)}) collective-permute-start(bf16[32,2048]{1,0:T(8,128)(2,1)S(1)} %get-tuple-element.62), channel_id=1, source_target_pairs={{0,12},{4,8},{8,4},{12,0},{1,13},{5,9},{9,5},{13,1},{2,14},{6,10},... | collective-permute-start | bytes 393224 | tf_op jit(solution)/shard_map/ppermute | solution.py:328
  107.0 2.1 %collective-permute-start.27 = (bf16[32,2048]{1,0:T(8,128)(2,1)S(1)}, bf16[32,2048]{1,0:T(8,128)(2,1)S(1)}, u32[]{:S(2)}, u32[]{:S(2)}) collective-permute-start(bf16[32,2048]{1,0:T(8,128)(2,1)S(1)} %get-tuple-element.64), channel_id=1, source_target_pairs={{0,8},{4,12},{8,0},{12,4},{1,9},{5,13},{9,1},{13,5},{2,10},{6,14},... | collective-permute-start | bytes 393224 | tf_op jit(solution)/shard_map/ppermute | solution.py:328
  109.1 3.8 %collective-permute-done.25.refs_0_ = bf16[32,2048]{1,0:T(8,128)(2,1)S(1)} collective-permute-done((bf16[32,2048]{1,0:T(8,128)(2,1)S(1)}, bf16[32,2048]{1,0:T(8,128)(2,1)S(1)}, u32[]{:S(2)}, u32[]{:S(2)}) %collective-permute-start.25) | collective-permute-done | bytes 131104 | tf_op jit(solution)/shard_map/ppermute | solution.py:328
  112.9 4.7 %collective-permute-done.26.refs_1_ = bf16[32,2048]{1,0:T(8,128)(2,1)S(1)} collective-permute-done((bf16[32,2048]{1,0:T(8,128)(2,1)S(1)}, bf16[32,2048]{1,0:T(8,128)(2,1)S(1)}, u32[]{:S(2)}, u32[]{:S(2)}) %collective-permute-start.26) | collective-permute-done | bytes 131104 | tf_op jit(solution)/shard_map/ppermute | solution.py:328
  117.9 0.8 shard_map.119
  (65 shorter events, 4.6 us)
Async XLA Ops:
  0.0 8.9 %collective-permute-start = (bf16[32,2048]{1,0:T(8,128)(2,1)}, bf16[32,2048]{1,0:T(8,128)(2,1)S(1)}, u32[]{:S(2)}, u32[]{:S(2)}) collective-permute-start(bf16[32,2048]{1,0:T(8,128)(2,1)} %q_hbm.1), channel_id=1, source_target_pairs={{0,4},{4,0},{8,12},{12,8},{1,5},{5,1},{9,13},{13,9},{2,6},{6,2},{1... | collective-permute-start | bytes 393224 | tf_op jit(solution)/shard_map/ppermute | solution.py:328
  3.1 15.9 %collective-permute-start.4 = (bf16[32,2048]{1,0:T(8,128)(2,1)}, bf16[32,2048]{1,0:T(8,128)(2,1)S(1)}, u32[]{:S(2)}, u32[]{:S(2)}) collective-permute-start(bf16[32,2048]{1,0:T(8,128)(2,1)} %q_hbm.1), channel_id=1, source_target_pairs={{0,12},{4,8},{8,4},{12,0},{1,13},{5,9},{9,5},{13,1},{2,14},{6,10},... | collective-permute-start | bytes 393224 | tf_op jit(solution)/shard_map/ppermute | solution.py:328
  5.5 12.1 %collective-permute-start.2 = (bf16[32,2048]{1,0:T(8,128)(2,1)}, bf16[32,2048]{1,0:T(8,128)(2,1)S(1)}, u32[]{:S(2)}, u32[]{:S(2)}) collective-permute-start(bf16[32,2048]{1,0:T(8,128)(2,1)} %q_hbm.1), channel_id=1, source_target_pairs={{0,8},{4,12},{8,0},{12,4},{1,9},{5,13},{9,1},{13,5},{2,10},{6,14},... | collective-permute-start | bytes 393224 | tf_op jit(solution)/shard_map/ppermute | solution.py:328
  10.1 36.2 %slice-start.12 = ((s8[8388608]{0:T(1024)(128)(4,1)}), s8[4194304]{0:T(1024)(128)(4,1)S(1)}, s32[]{:S(2)}) async-start(s8[8388608]{0:T(1024)(128)(4,1)} %bitcast.12), calls=%async_computation.12 | async-start | bytes 8388608
  10.1 12.8 %collective-permute-start.1 = (bf16[32,2176]{1,0:T(8,128)(2,1)S(1)}, bf16[32,2176]{1,0:T(8,128)(2,1)S(1)}, u32[]{:S(2)}, u32[]{:S(2)}) collective-permute-start(bf16[32,2176]{1,0:T(8,128)(2,1)S(1)} %shard_map.101), channel_id=1, source_target_pairs={{0,4},{4,0},{8,12},{12,8},{1,5},{5,1},{9,13},{13,9},{2,6},{6,2},{1... | collective-permute-start | bytes 417800 | tf_op jit(solution)/shard_map/ppermute | solution.py:328
  18.9 27.4 %slice-start.13 = ((s8[8388608]{0:T(1024)(128)(4,1)}), s8[4194304]{0:T(1024)(128)(4,1)S(1)}, s32[]{:S(2)}) async-start(s8[8388608]{0:T(1024)(128)(4,1)} %bitcast.12), calls=%async_computation.13 | async-start | bytes 8388608
  18.9 11.7 %collective-permute-start.3 = (bf16[32,2176]{1,0:T(8,128)(2,1)S(1)}, bf16[32,2176]{1,0:T(8,128)(2,1)S(1)}, u32[]{:S(2)}, u32[]{:S(2)}) collective-permute-start(bf16[32,2176]{1,0:T(8,128)(2,1)S(1)} %shard_map.102), channel_id=1, source_target_pairs={{0,8},{4,12},{8,0},{12,4},{1,9},{5,13},{9,1},{13,5},{2,10},{6,14},... | collective-permute-start | bytes 417800 | tf_op jit(solution)/shard_map/ppermute | solution.py:328
  20.2 10.3 %collective-permute-start.5 = (bf16[32,2176]{1,0:T(8,128)(2,1)S(1)}, bf16[32,2176]{1,0:T(8,128)(2,1)S(1)}, u32[]{:S(2)}, u32[]{:S(2)}) collective-permute-start(bf16[32,2176]{1,0:T(8,128)(2,1)S(1)} %shard_map.103), channel_id=1, source_target_pairs={{0,12},{4,8},{8,4},{12,0},{1,13},{5,9},{9,5},{13,1},{2,14},{6,10},... | collective-permute-start | bytes 417800 | tf_op jit(solution)/shard_map/ppermute | solution.py:328
  31.0 24.9 %copy-start = (bf16[32,2048]{1,0:T(8,128)(2,1)S(1)}, bf16[32,2048]{1,0:T(8,128)(2,1)}, u32[]{:S(2)}) copy-start(bf16[32,2048]{1,0:T(8,128)(2,1)} %stream_ref.1) | copy-start | bytes 393220
  31.1 7.5 %collective-permute-start.8 = (bf16[32,2048]{1,0:T(8,128)(2,1)S(1)}, bf16[32,2048]{1,0:T(8,128)(2,1)S(1)}, u32[]{:S(2)}, u32[]{:S(2)}) collective-permute-start(bf16[32,2048]{1,0:T(8,128)(2,1)S(1)} %shard_map.104.refs_0_), channel_id=1, source_target_pairs={{0,12},{4,8},{8,4},{12,0},{1,13},{5,9},{9,5},{13,1},{2,14},{6,10},... | collective-permute-start | bytes 393224 | tf_op jit(solution)/shard_map/ppermute | solution.py:328
  32.6 13.7 %collective-permute-start.7 = (bf16[32,2048]{1,0:T(8,128)(2,1)S(1)}, bf16[32,2048]{1,0:T(8,128)(2,1)S(1)}, u32[]{:S(2)}, u32[]{:S(2)}) collective-permute-start(bf16[32,2048]{1,0:T(8,128)(2,1)S(1)} %shard_map.104.refs_0_), channel_id=1, source_target_pairs={{0,8},{4,12},{8,0},{12,4},{1,9},{5,13},{9,1},{13,5},{2,10},{6,14},... | collective-permute-start | bytes 393224 | tf_op jit(solution)/shard_map/ppermute | solution.py:328
  35.8 10.4 %collective-permute-start.6 = (bf16[32,2048]{1,0:T(8,128)(2,1)S(1)}, bf16[32,2048]{1,0:T(8,128)(2,1)S(1)}, u32[]{:S(2)}, u32[]{:S(2)}) collective-permute-start(bf16[32,2048]{1,0:T(8,128)(2,1)S(1)} %shard_map.104.refs_0_), channel_id=1, source_target_pairs={{0,4},{4,0},{8,12},{12,8},{1,5},{5,1},{9,13},{13,9},{2,6},{6,2},{1... | collective-permute-start | bytes 393224 | tf_op jit(solution)/shard_map/ppermute | solution.py:328
  48.2 1.6 %collective-permute-start.9 = (bf16[64,2048]{1,0:T(8,128)(2,1)S(1)}, bf16[64,2048]{1,0:T(8,128)(2,1)S(1)}, u32[]{:S(2)}, u32[]{:S(2)}) collective-permute-start(bf16[64,2048]{1,0:T(8,128)(2,1)S(1)} %get-tuple-element.39), channel_id=1, source_target_pairs={{0,1},{1,0},{2,3},{3,2},{4,5},{5,4},{6,7},{7,6},{8,9},{9,8},{10,11... | collective-permute-start | bytes 786440 | tf_op jit(solution)/shard_map/ppermute | solution.py:324
  50.4 14.0 %copy-start.1 = (f32[8192]{0:T(1024)S(1)}, f32[8192]{0:T(1024)}, u32[]{:S(2)}) copy-start(f32[8192]{0:T(1024)} %param.16) | copy-start | bytes 98308
  50.4 5.6 %collective-permute-start.10 = (bf16[32,2048]{1,0:T(8,128)(2,1)S(1)}, bf16[32,2048]{1,0:T(8,128)(2,1)S(1)}, u32[]{:S(2)}, u32[]{:S(2)}) collective-permute-start(bf16[32,2048]{1,0:T(8,128)(2,1)S(1)} %get-tuple-element.41), channel_id=1, source_target_pairs={{0,2},{2,0},{1,3},{3,1},{4,6},{6,4},{5,7},{7,5},{8,10},{10,8},{9,1... | collective-permute-start | bytes 393224 | tf_op jit(solution)/shard_map/ppermute | solution.py:324
  56.0 11.0 %slice-start.4 = ((s8[14680064]{0:T(1024)(128)(4,1)}), s8[2097152]{0:T(1024)(128)(4,1)S(1)}, s32[]{:S(2)}) async-start(s8[14680064]{0:T(1024)(128)(4,1)} %bitcast.8), calls=%async_computation.4 | async-start | bytes 4194304
  56.0 11.0 %slice-start.5 = ((s8[14680064]{0:T(1024)(128)(4,1)}), s8[4194304]{0:T(1024)(128)(4,1)S(1)}, s32[]{:S(2)}) async-start(s8[14680064]{0:T(1024)(128)(4,1)} %bitcast.8), calls=%async_computation.5 | async-start | bytes 8388608
  56.0 8.3 %collective-permute-start.14 = (bf16[32,2048]{1,0:T(8,128)(2,1)S(1)}, bf16[32,2048]{1,0:T(8,128)(2,1)S(1)}, u32[]{:S(2)}, u32[]{:S(2)}) collective-permute-start(bf16[32,2048]{1,0:T(8,128)(2,1)S(1)} %shard_map.107), channel_id=1, source_target_pairs={{0,12},{1,8},{2,4},{3,0},{4,13},{5,9},{6,5},{7,1},{8,14},{9,10},{1... | collective-permute-start | bytes 393224 | tf_op jit(solution)/shard_map/ppermute | solution.py:412
  57.4 7.6 %collective-permute-start.13 = (bf16[32,2048]{1,0:T(8,128)(2,1)S(1)}, bf16[32,2048]{1,0:T(8,128)(2,1)S(1)}, u32[]{:S(2)}, u32[]{:S(2)}) collective-permute-start(bf16[32,2048]{1,0:T(8,128)(2,1)S(1)} %shard_map.107), channel_id=1, source_target_pairs={{0,8},{1,12},{2,0},{3,4},{4,9},{5,13},{6,1},{7,5},{8,10},{9,14},{1... | collective-permute-start | bytes 393224 | tf_op jit(solution)/shard_map/ppermute | solution.py:412
  58.9 6.8 %collective-permute-start.12 = (bf16[32,2048]{1,0:T(8,128)(2,1)S(1)}, bf16[32,2048]{1,0:T(8,128)(2,1)S(1)}, u32[]{:S(2)}, u32[]{:S(2)}) collective-permute-start(bf16[32,2048]{1,0:T(8,128)(2,1)S(1)} %shard_map.107), channel_id=1, source_target_pairs={{0,4},{1,0},{2,12},{3,8},{4,5},{5,1},{6,13},{7,9},{8,6},{9,2},{10,... | collective-permute-start | bytes 393224 | tf_op jit(solution)/shard_map/ppermute | solution.py:412
  58.9 7.4 %collective-permute-start.11 = (bf16[32,2048]{1,0:T(8,128)(2,1)S(1)}, bf16[32,2048]{1,0:T(8,128)(2,1)S(1)}, u32[]{:S(2)}, u32[]{:S(2)}) collective-permute-start(bf16[32,2048]{1,0:T(8,128)(2,1)S(1)} %shard_map.107), channel_id=1, source_target_pairs={{0,0},{1,4},{2,8},{3,12},{4,1},{5,5},{6,9},{7,13},{8,2},{9,6},{10,... | collective-permute-start | bytes 393224 | tf_op jit(solution)/shard_map/ppermute | solution.py:412
  65.0 2.2 %slice-start = ((s8[14680064]{0:T(1024)(128)(4,1)}), s8[4194304]{0:T(1024)(128)(4,1)S(1)}, s32[]{:S(2)}) async-start(s8[14680064]{0:T(1024)(128)(4,1)} %bitcast.6), calls=%async_computation | async-start | bytes 8388608
  65.0 3.5 %slice-start.1 = ((s8[14680064]{0:T(1024)(128)(4,1)}), s8[4194304]{0:T(1024)(128)(4,1)S(1)}, s32[]{:S(2)}) async-start(s8[14680064]{0:T(1024)(128)(4,1)} %bitcast.6), calls=%async_computation.1 | async-start | bytes 8388608
  65.0 4.7 %slice-start.6 = ((s8[14680064]{0:T(1024)(128)(4,1)}), s8[4194304]{0:T(1024)(128)(4,1)S(1)}, s32[]{:S(2)}) async-start(s8[14680064]{0:T(1024)(128)(4,1)} %bitcast.8), calls=%async_computation.6 | async-start | bytes 8388608
  65.7 5.3 %slice-start.2 = ((s8[14680064]{0:T(1024)(128)(4,1)}), s8[4194304]{0:T(1024)(128)(4,1)S(1)}, s32[]{:S(2)}) async-start(s8[14680064]{0:T(1024)(128)(4,1)} %bitcast.6), calls=%async_computation.2 | async-start | bytes 8388608
  65.7 6.5 %slice-start.7 = ((s8[14680064]{0:T(1024)(128)(4,1)}), s8[4194304]{0:T(1024)(128)(4,1)S(1)}, s32[]{:S(2)}) async-start(s8[14680064]{0:T(1024)(128)(4,1)} %bitcast.8), calls=%async_computation.7 | async-start | bytes 8388608
  66.4 6.5 %slice-start.3 = ((s8[14680064]{0:T(1024)(128)(4,1)}), s8[2097152]{0:T(1024)(128)(4,1)S(1)}, s32[]{:S(2)}) async-start(s8[14680064]{0:T(1024)(128)(4,1)} %bitcast.6), calls=%async_computation.3 | async-start | bytes 4194304
  75.8 2.8 %collective-permute-start.15 = (bf16[64,3840]{1,0:T(8,128)(2,1)S(1)}, bf16[64,3840]{1,0:T(8,128)(2,1)S(1)}, u32[]{:S(2)}, u32[]{:S(2)}) collective-permute-start(bf16[64,3840]{1,0:T(8,128)(2,1)S(1)} %get-tuple-element.51), channel_id=1, source_target_pairs={{0,1},{1,0},{2,3},{3,2},{4,5},{5,4},{6,7},{7,6},{8,9},{9,8},{10,11... | collective-permute-start | bytes 1474568 | tf_op jit(solution)/shard_map/ppermute | solution.py:324
  78.0 5.8 %collective-permute-start.17 = (bf16[64,3584]{1,0:T(8,128)(2,1)S(1)}, bf16[64,3584]{1,0:T(8,128)(2,1)S(1)}, u32[]{:S(2)}, u32[]{:S(2)}) collective-permute-start(bf16[64,3584]{1,0:T(8,128)(2,1)S(1)} %get-tuple-element.58), channel_id=1, source_target_pairs={{0,1},{1,0},{2,3},{3,2},{4,5},{5,4},{6,7},{7,6},{8,9},{9,8},{10,11... | collective-permute-start | bytes 1376264 | tf_op jit(solution)/shard_map/ppermute | solution.py:324
  79.2 11.4 %collective-permute-start.16 = (bf16[32,3840]{1,0:T(8,128)(2,1)S(1)}, bf16[32,3840]{1,0:T(8,128)(2,1)S(1)}, u32[]{:S(2)}, u32[]{:S(2)}) collective-permute-start(bf16[32,3840]{1,0:T(8,128)(2,1)S(1)} %get-tuple-element.53), channel_id=1, source_target_pairs={{0,2},{2,0},{1,3},{3,1},{4,6},{6,4},{5,7},{7,5},{8,10},{10,8},{9,1... | collective-permute-start | bytes 737288 | tf_op jit(solution)/shard_map/ppermute | solution.py:324
  83.8 18.0 %slice-start.8 = ((s8[14680064]{0:T(1024)(128)(4,1)}), s8[2097152]{0:T(1024)(128)(4,1)S(1)}, s32[]{:S(2)}) async-start(s8[14680064]{0:T(1024)(128)(4,1)} %bitcast.10), calls=%async_computation.8 | async-start | bytes 4194304
  83.8 18.0 %slice-start.9 = ((s8[14680064]{0:T(1024)(128)(4,1)}), s8[4194304]{0:T(1024)(128)(4,1)S(1)}, s32[]{:S(2)}) async-start(s8[14680064]{0:T(1024)(128)(4,1)} %bitcast.10), calls=%async_computation.9 | async-start | bytes 8388608
  84.5 11.1 %collective-permute-start.18 = (bf16[32,3584]{1,0:T(8,128)(2,1)S(1)}, bf16[32,3584]{1,0:T(8,128)(2,1)S(1)}, u32[]{:S(2)}, u32[]{:S(2)}) collective-permute-start(bf16[32,3584]{1,0:T(8,128)(2,1)S(1)} %get-tuple-element.60), channel_id=1, source_target_pairs={{0,2},{2,0},{1,3},{3,1},{4,6},{6,4},{5,7},{7,5},{8,10},{10,8},{9,1... | collective-permute-start | bytes 688136 | tf_op jit(solution)/shard_map/ppermute | solution.py:324
  90.6 11.2 %slice-start.10 = ((s8[14680064]{0:T(1024)(128)(4,1)}), s8[4194304]{0:T(1024)(128)(4,1)S(1)}, s32[]{:S(2)}) async-start(s8[14680064]{0:T(1024)(128)(4,1)} %bitcast.10), calls=%async_computation.10 | async-start | bytes 8388608
  90.8 7.5 %collective-permute-start.21 = (bf16[32,1792]{1,0:T(8,128)(2,1)S(1)}, bf16[32,1792]{1,0:T(8,128)(2,1)S(1)}, u32[]{:S(2)}, u32[]{:S(2)}) collective-permute-start(bf16[32,1792]{1,0:T(8,128)(2,1)S(1)} %get-tuple-element.54.refs_0_), channel_id=1, source_target_pairs={{0,2},{2,0},{1,3},{3,1},{4,6},{6,4},{5,7},{7,5},{8,10},{10,8},{9,1... | collective-permute-start | bytes 344072 | tf_op jit(solution)/shard_map/ppermute | solution.py:324
  95.6 6.3 %slice-start.11 = ((s8[14680064]{0:T(1024)(128)(4,1)}), s8[4194304]{0:T(1024)(128)(4,1)S(1)}, s32[]{:S(2)}) async-start(s8[14680064]{0:T(1024)(128)(4,1)} %bitcast.10), calls=%async_computation.11 | async-start | bytes 8388608
  95.7 4.9 %collective-permute-start.22 = (bf16[32,1792]{1,0:T(8,128)(2,1)S(1)}, bf16[32,1792]{1,0:T(8,128)(2,1)S(1)}, u32[]{:S(2)}, u32[]{:S(2)}) collective-permute-start(bf16[32,1792]{1,0:T(8,128)(2,1)S(1)} %shard_map.117.refs_1_), channel_id=1, source_target_pairs={{0,2},{2,0},{1,3},{3,1},{4,6},{6,4},{5,7},{7,5},{8,10},{10,8},{9,1... | collective-permute-start | bytes 344072 | tf_op jit(solution)/shard_map/ppermute | solution.py:324
  97.8 2.8 %collective-permute-start.19 = (bf16[32,1792]{1,0:T(8,128)(2,1)S(1)}, bf16[32,1792]{1,0:T(8,128)(2,1)S(1)}, u32[]{:S(2)}, u32[]{:S(2)}) collective-permute-start(bf16[32,1792]{1,0:T(8,128)(2,1)S(1)} %get-tuple-element.54.refs_0_), channel_id=1, source_target_pairs={{0,1},{1,0},{2,3},{3,2},{4,5},{5,4},{6,7},{7,6},{8,9},{9,8},{10,11... | collective-permute-start | bytes 344072 | tf_op jit(solution)/shard_map/ppermute | solution.py:324
  97.8 2.8 %collective-permute-start.20 = (bf16[32,1792]{1,0:T(8,128)(2,1)S(1)}, bf16[32,1792]{1,0:T(8,128)(2,1)S(1)}, u32[]{:S(2)}, u32[]{:S(2)}) collective-permute-start(bf16[32,1792]{1,0:T(8,128)(2,1)S(1)} %shard_map.117.refs_1_), channel_id=1, source_target_pairs={{0,1},{1,0},{2,3},{3,2},{4,5},{5,4},{6,7},{7,6},{8,9},{9,8},{10,11... | collective-permute-start | bytes 344072 | tf_op jit(solution)/shard_map/ppermute | solution.py:324
  98.3 2.3 %collective-permute-start.23 = (bf16[32,1792]{1,0:T(8,128)(2,1)S(1)}, bf16[32,1792]{1,0:T(8,128)(2,1)S(1)}, u32[]{:S(2)}, u32[]{:S(2)}) collective-permute-start(bf16[32,1792]{1,0:T(8,128)(2,1)S(1)} %collective-permute-done.21.refs_4_), channel_id=1, source_target_pairs={{0,1},{1,0},{2,3},{3,2},{4,5},{5,4},{6,7},{7,6},{8,9},{9,8},{10,11... | collective-permute-start | bytes 344072 | tf_op jit(solution)/shard_map/ppermute | solution.py:324
  100.6 1.3 %collective-permute-start.24 = (bf16[32,1792]{1,0:T(8,128)(2,1)S(1)}, bf16[32,1792]{1,0:T(8,128)(2,1)S(1)}, u32[]{:S(2)}, u32[]{:S(2)}) collective-permute-start(bf16[32,1792]{1,0:T(8,128)(2,1)S(1)} %collective-permute-done.22.refs_5_), channel_id=1, source_target_pairs={{0,1},{1,0},{2,3},{3,2},{4,5},{5,4},{6,7},{7,6},{8,9},{9,8},{10,11... | collective-permute-start | bytes 344072 | tf_op jit(solution)/shard_map/ppermute | solution.py:324
  104.6 8.3 %collective-permute-start.25 = (bf16[32,2048]{1,0:T(8,128)(2,1)S(1)}, bf16[32,2048]{1,0:T(8,128)(2,1)S(1)}, u32[]{:S(2)}, u32[]{:S(2)}) collective-permute-start(bf16[32,2048]{1,0:T(8,128)(2,1)S(1)} %get-tuple-element.62), channel_id=1, source_target_pairs={{0,12},{4,8},{8,4},{12,0},{1,13},{5,9},{9,5},{13,1},{2,14},{6,10},... | collective-permute-start | bytes 393224 | tf_op jit(solution)/shard_map/ppermute | solution.py:328
  107.0 10.6 %collective-permute-start.26 = (bf16[32,2048]{1,0:T(8,128)(2,1)S(1)}, bf16[32,2048]{1,0:T(8,128)(2,1)S(1)}, u32[]{:S(2)}, u32[]{:S(2)}) collective-permute-start(bf16[32,2048]{1,0:T(8,128)(2,1)S(1)} %get-tuple-element.63), channel_id=1, source_target_pairs={{0,4},{4,0},{8,12},{12,8},{1,5},{5,1},{9,13},{13,9},{2,6},{6,2},{1... | collective-permute-start | bytes 393224 | tf_op jit(solution)/shard_map/ppermute | solution.py:328
  107.0 10.9 %collective-permute-start.27 = (bf16[32,2048]{1,0:T(8,128)(2,1)S(1)}, bf16[32,2048]{1,0:T(8,128)(2,1)S(1)}, u32[]{:S(2)}, u32[]{:S(2)}) collective-permute-start(bf16[32,2048]{1,0:T(8,128)(2,1)S(1)} %get-tuple-element.64), channel_id=1, source_target_pairs={{0,8},{4,12},{8,0},{12,4},{1,9},{5,13},{9,1},{13,5},{2,10},{6,14},... | collective-permute-start | bytes 393224 | tf_op jit(solution)/shard_map/ppermute | solution.py:328

commit v2 on v1

--- a/solution.py
+++ b/solution.py
@@ -90,7 +90,8 @@
     )
     allowed = [ahead <= limit for limit in limits]
     head_lane = lax.broadcasted_iota(jnp.int32, (rows, LANES), 1)
-    lse_tile = jnp.zeros((rows, LANES), F32)
+    peak_tile = jnp.zeros((rows, LANES), F32)
+    total_tile = jnp.ones((rows, LANES), F32)
     for kv in range(kv_dev):
         stacked = jnp.concatenate(
             [q_ref[:, (kv * group + h) * DH : (kv * group + h + 1) * DH] for h in range(group)], axis=0
@@ -102,7 +103,6 @@
             preferred_element_type=F32,
         )
     for kv in range(kv_dev):
-        totals = []
         for h in range(group):
             head = kv * group + h
             span = slice(h * rows, (h + 1) * rows)
@@ -115,16 +115,19 @@
             row_total = jnp.sum(functools.reduce(jnp.add, parts), axis=1, keepdims=True)
             for slot, p in enumerate(parts):
                 weight_ref[kv, span, slot * KB : (slot + 1) * KB] = p.astype(BF16)
-            totals.append(1.0 / row_total)
-            lse_tile = jnp.where(head_lane == head, peak * scale + jnp.log(row_total), lse_tile)
+            peak_tile = jnp.where(head_lane == head, peak, peak_tile)
+            total_tile = jnp.where(head_lane == head, row_total, total_tile)
+    inverse = 1.0 / total_tile
+    for kv in range(kv_dev):
         mixture = jnp.dot(
             weight_ref[kv], value_ref[:, kv * DH : (kv + 1) * DH], preferred_element_type=F32
         )
         for h in range(group):
             head = kv * group + h
             out_ref[:, head * DH : (head + 1) * DH] = (
-                mixture[h * rows : (h + 1) * rows] * totals[h]
+                mixture[h * rows : (h + 1) * rows] * inverse[:, head : head + 1]
             ).astype(BF16)
+    lse_tile = peak_tile * scale + jnp.log(total_tile)
     high = lse_tile.astype(BF16).astype(F32)
     rest = lse_tile - high
     mid = rest.astype(BF16).astype(F32)
@@ -290,23 +293,35 @@
     hidden_kernel(scale_ref, keep_ref, got_ref, out_ref)
 
 
-def down_kernel(n_chunk, tile, meta_ref, *refs):
-    pieces = refs[: 4 * n_chunk]
-    weight_ref, own_ref = refs[4 * n_chunk : 4 * n_chunk + 2]
-    sends, rows_ref = refs[4 * n_chunk + 2 : -1], refs[-1]
+def gather_rows(meta_ref, pieces, rows_ref):
     rows = pieces[0].shape[0]
-    shard, place = meta_ref[0], meta_ref[3]
-    for n in range(4):
-        at = pl.ds(pl.multiple_of((shard ^ place ^ n) * rows, rows), rows)
-        start = 0
-        for c in range(n_chunk):
-            piece = pieces[n * n_chunk + c]
-            rows_ref[at, start : start + piece.shape[1]] = piece[...]
-            start += piece.shape[1]
-
+    for n, piece in enumerate(pieces):
+        at = pl.ds(pl.multiple_of((meta_ref[0] ^ meta_ref[3] ^ n) * rows, rows), rows)
+        rows_ref[at, :] = piece[...]
+
+
+def first_down_kernel(tile, meta_ref, *refs):
+    pieces, (weight_ref, out_ref, rows_ref) = refs[:4], refs[4:]
+    gather_rows(meta_ref, pieces, rows_ref)
+    depth = rows_ref.shape[1]
+    for at in range(0, weight_ref.shape[1], tile):
+        out_ref[:, at : at + tile] = jnp.dot(
+            rows_ref[...], weight_ref[:depth, at : at + tile], preferred_element_type=F32
+        )
+
+
+def down_kernel(tile, meta_ref, *refs):
+    pieces, (weight_ref, so_far_ref, own_ref) = refs[:4], refs[4:7]
+    sends, rows_ref = refs[7:-1], refs[-1]
+    gather_rows(meta_ref, pieces, rows_ref)
+    rows = pieces[0].shape[0]
+    depth = rows_ref.shape[1]
+    start = weight_ref.shape[0] - depth
     for at in range(0, weight_ref.shape[1], tile):
         columns = slice(at, at + tile)
-        part = jnp.dot(rows_ref[...], weight_ref[:, columns], preferred_element_type=F32)
+        part = so_far_ref[:, columns] + jnp.dot(
+            rows_ref[...], weight_ref[start:, columns], preferred_element_type=F32
+        )
         own_ref[:, columns] = part[:rows]
         for n, send in enumerate(sends):
             send[:, columns] = part[(n + 1) * rows : (n + 2) * rows].astype(BF16)
@@ -352,7 +367,7 @@
     total = rows * n_context
     blocks = key_cache.shape[0] // KB
     kv_width = key_cache.shape[1]
-    order = (3, 1, 2)
+    order = (3, 2, 1)
 
     got_q = {m: turn(queries, "ctx", n_context, m) for m in order}
     picked = struct((MOST * KB, kv_width), BF16)
@@ -396,6 +411,7 @@
         [SM] + [VM] * 5,
         (meta,) + tuple(attention[m] for m in range(4)) + (in_vmem(out_weight),),
         scratch=[pltpu.VMEM((total, heads_width), BF16)],
+        cost=6,
     )
     got = swap(away, "sec")
     keep, away = call(
@@ -431,6 +447,7 @@
             (struct((rows, width), BF16), struct((rows, LANES), F32)),
             [SM, VM, VM],
             (meta, all_middle[m], norm_gain[None]),
+            cost=0,
         )
         for m in range(4)
     ]
@@ -480,17 +497,21 @@
         across = swap(own, "head")
         beside = swap(own, "sec")
         hidden.append((own, beside, across, swap(across, "sec")))
-    n_chunk = len(chunks)
-
     out_width = down_weight.shape[1]
+    down_vmem = in_vmem(down_weight)
+    so_far = call(
+        functools.partial(first_down_kernel, 512),
+        struct((total, out_width), F32),
+        [SM] + [VM] * 5,
+        (meta,) + hidden[0] + (down_vmem,),
+        scratch=[pltpu.VMEM((total, chunks[0][1]), BF16)],
+    )
     res = call(
-        functools.partial(down_kernel, n_chunk, 512),
+        functools.partial(down_kernel, 512),
         (struct((rows, out_width), F32),) + (struct((rows, out_width), BF16),) * 3,
-        [SM] + [VM] * (4 * n_chunk + 1),
-        (meta,)
-        + tuple(hidden[c][n] for n in range(4) for c in range(n_chunk))
-        + (in_vmem(down_weight),),
-        scratch=[pltpu.VMEM((total, hidden_width), BF16)],
+        [SM] + [VM] * 6,
+        (meta,) + hidden[1] + (down_vmem, so_far),
+        scratch=[pltpu.VMEM((total, chunks[1][1]), BF16)],
     )
     parts = [turn(res[m], "ctx", n_context, m) for m in order]
     return call(

time: 119 us -> 117 us (0.983)
  local copies, waits for them, and re-layouts: 6.61 us -> 0.81 us
  starting transfers between devices: 35.4 us -> 39.1 us
  waiting for transfers between devices: 54.6 us -> 53.3 us
  Pallas kernels: 21.9 us -> 23.1 us
    unnamed x32, local copies, waits for them, and re-layouts: 5.88 us -> 0.07 us
    ppermute x4, starting transfers between devices: 3.55 us -> 7.11 us  [direct_body(): lax.ppermute(middle, ALL, [(a * n_context + b, (b ^ m) * n_context + a) f...]
    ppermute x12, starting transfers between devices: 12.3 us -> 14 us  [swap(): return lax.ppermute(x, axis, [(0, 1), (1, 0)])]
    ppermute x12, starting transfers between devices: 19.5 us -> 18 us  [turn(): return lax.ppermute(x, axis, [(i, i ^ offset) for i in range(n)])]
    ppermute x12, waiting for transfers between devices: 17.2 us -> 15.9 us  [swap(): return lax.ppermute(x, axis, [(0, 1), (1, 0)])]
    ppermute x4, waiting for transfers between devices: 4.76 us -> 5.99 us  [direct_body(): lax.ppermute(middle, ALL, [(a * n_context + b, (b ^ m) * n_context + a) f...]
    ppermute x12, waiting for transfers between devices: 32.6 us -> 31.4 us  [turn(): return lax.ppermute(x, axis, [(i, i ^ offset) for i in range(n)])]
    pallas_call x20 -> x21, Pallas kernels: 21.9 us -> 23.1 us  [call(): pl.pallas_call(kernel, out_shape=out, in_specs=in_specs, out_specs=jax.tr...]
  transfers between devices with their start and end apart: 28 -> 28, of which waited for: 14 -> 12; matrix products, arithmetic and copies ran while one was open for 1% -> 1% of each run, Pallas kernels for 10% -> 12%
where the time goes in v2:
time: 117 us
  waiting for transfers between devices  53.3 us (46%)
  starting transfers between devices  39.1 us (33%)
  Pallas kernels  23.1 us (20%)
    ppermute x12, waiting for transfers between devices, turn(): return lax.ppermute(x, axis, [(i, i ^ offset) for i in range(n)])  31.4 us
    pallas_call x21, Pallas kernels, call(): pl.pallas_call(kernel, out_shape=out, in_specs=in_specs, out_specs=jax.tr...  23.1 us
    ppermute x12, starting transfers between devices, turn(): return lax.ppermute(x, axis, [(i, i ^ offset) for i in range(n)])  18 us
    ppermute x12, waiting for transfers between devices, swap(): return lax.ppermute(x, axis, [(0, 1), (1, 0)])  15.9 us
    ppermute x12, starting transfers between devices, swap(): return lax.ppermute(x, axis, [(0, 1), (1, 0)])  14 us
    ppermute x4, starting transfers between devices, direct_body(): lax.ppermute(middle, ALL, [(a * n_context + b, (b ^ m) * n_context + a) f...  7.11 us
    ppermute x4, waiting for transfers between devices, direct_body(): lax.ppermute(middle, ALL, [(a * n_context + b, (b ^ m) * n_context + a) f...  5.99 us
  transfers between devices with their start and end apart: 28, of which 12 were waited for; matrix products, arithmetic and copies ran while one was open for 1% of the time, Pallas kernels for 12%

profile of v2, /device:TPU:0, one launch (start us, length us, event | category | flops | bytes accessed | tf_op | source)
XLA Modules:
  0.0 116.6 jit_solution(10746308532915104786)
XLA Ops:
  0.0 3.1 %collective-permute-start = (bf16[32,2048]{1,0:T(8,128)(2,1)}, bf16[32,2048]{1,0:T(8,128)(2,1)S(1)}, u32[]{:S(2)}, u32[]{:S(2)}) collective-permute-start(bf16[32,2048]{1,0:T(8,128)(2,1)} %q_hbm.1), channel_id=1, source_target_pairs={{0,4},{4,0},{8,12},{12,8},{1,5},{5,1},{9,13},{13,9},{2,6},{6,2},{1... | collective-permute-start | bytes 393224 | tf_op jit(solution)/shard_map/ppermute | solution.py:343
  3.1 2.6 %collective-permute-start.2 = (bf16[32,2048]{1,0:T(8,128)(2,1)}, bf16[32,2048]{1,0:T(8,128)(2,1)S(1)}, u32[]{:S(2)}, u32[]{:S(2)}) collective-permute-start(bf16[32,2048]{1,0:T(8,128)(2,1)} %q_hbm.1), channel_id=1, source_target_pairs={{0,8},{4,12},{8,0},{12,4},{1,9},{5,13},{9,1},{13,5},{2,10},{6,14},... | collective-permute-start | bytes 393224 | tf_op jit(solution)/shard_map/ppermute | solution.py:343
  5.6 0.7 concatenate.3.meta_ref
  6.4 2.6 %shard_map.100 = (bf16[512,256]{1,0:T(8,128)(2,1)S(1)}, bf16[512,256]{1,0:T(8,128)(2,1)S(1)}, bf16[32,2176]{1,0:T(8,128)(2,1)S(1)}) custom-call(s32[12]{0:T(128)S(1)} %concatenate.3.meta_ref, bf16[32,2048]{1,0:T(8,128)(2,1)} %q_hbm.1, bf16[2048,256]{1,0:T(8,128)(2,1)} %key_hbm.1, bf16[2048,256]{1,0:T(8,128)(2,1)} %value_hbm.1), custom_call_target="tpu_custom_call" | custom-call | flops 3000000000 | bytes 2891824 | tf_op jit(solution)/shard_map/pallas_call | solution.py:37
  9.0 1.4 %shard_map.101 = bf16[32,2176]{1,0:T(8,128)(2,1)S(1)} custom-call(s32[12]{0:T(128)S(1)} %concatenate.3.meta_ref, bf16[32,2048]{1,0:T(8,128)(2,1)S(1)} %collective-permute-done.q_ref, bf16[512,256]{1,0:T(8,128)(2,1)S(1)} %get-tuple-element.36.key_ref, bf16[512,256]{1,0:T(8,128)(2,1)S(1)} %get-tuple-element.37.value_ref), custom_call_target="tpu_custom_call" | custom-call | flops 3000000000 | bytes 794672 | tf_op jit(solution)/shard_map/pallas_call | solution.py:37
  10.3 1.0 collective-permute-start.1
  11.3 4.9 %collective-permute-done.2.q_ref = bf16[32,2048]{1,0:T(8,128)(2,1)S(1)} collective-permute-done((bf16[32,2048]{1,0:T(8,128)(2,1)}, bf16[32,2048]{1,0:T(8,128)(2,1)S(1)}, u32[]{:S(2)}, u32[]{:S(2)}) %collective-permute-start.2) | collective-permute-done | bytes 131104 | tf_op jit(solution)/shard_map/ppermute | solution.py:343
  16.2 1.3 %shard_map.102 = bf16[32,2176]{1,0:T(8,128)(2,1)S(1)} custom-call(s32[12]{0:T(128)S(1)} %concatenate.3.meta_ref, bf16[32,2048]{1,0:T(8,128)(2,1)S(1)} %collective-permute-done.2.q_ref, bf16[512,256]{1,0:T(8,128)(2,1)S(1)} %get-tuple-element.36.key_ref, bf16[512,256]{1,0:T(8,128)(2,1)S(1)} %get-tuple-element.37.value_ref), custom_call_target="tpu_custom_call" | custom-call | flops 3000000000 | bytes 794672 | tf_op jit(solution)/shard_map/pallas_call | solution.py:37
  17.6 1.4 %shard_map.103 = bf16[32,2176]{1,0:T(8,128)(2,1)S(1)} custom-call(s32[12]{0:T(128)S(1)} %concatenate.3.meta_ref, bf16[32,2048]{1,0:T(8,128)(2,1)S(1)} %collective-permute-done.4.q_ref, bf16[512,256]{1,0:T(8,128)(2,1)S(1)} %get-tuple-element.36.key_ref, bf16[512,256]{1,0:T(8,128)(2,1)S(1)} %get-tuple-element.37.value_ref), custom_call_target="tpu_custom_call" | custom-call | flops 3000000000 | bytes 794672 | tf_op jit(solution)/shard_map/pallas_call | solution.py:37
  19.0 2.3 %collective-permute-start.5 = (bf16[32,2176]{1,0:T(8,128)(2,1)S(1)}, bf16[32,2176]{1,0:T(8,128)(2,1)S(1)}, u32[]{:S(2)}, u32[]{:S(2)}) collective-permute-start(bf16[32,2176]{1,0:T(8,128)(2,1)S(1)} %shard_map.103), channel_id=1, source_target_pairs={{0,12},{4,8},{8,4},{12,0},{1,13},{5,9},{9,5},{13,1},{2,14},{6,10},... | collective-permute-start | bytes 417800 | tf_op jit(solution)/shard_map/ppermute | solution.py:343
  21.3 6.8 %collective-permute-done.3.refs_2_ = bf16[32,2176]{1,0:T(8,128)(2,1)S(1)} collective-permute-done((bf16[32,2176]{1,0:T(8,128)(2,1)S(1)}, bf16[32,2176]{1,0:T(8,128)(2,1)S(1)}, u32[]{:S(2)}, u32[]{:S(2)}) %collective-permute-start.3) | collective-permute-done | bytes 139296 | tf_op jit(solution)/shard_map/ppermute | solution.py:343
  28.6 2.1 %collective-permute-start.6 = (bf16[32,2048]{1,0:T(8,128)(2,1)S(1)}, bf16[32,2048]{1,0:T(8,128)(2,1)S(1)}, u32[]{:S(2)}, u32[]{:S(2)}) collective-permute-start(bf16[32,2048]{1,0:T(8,128)(2,1)S(1)} %shard_map.104.refs_0_), channel_id=1, source_target_pairs={{0,4},{4,0},{8,12},{12,8},{1,5},{5,1},{9,13},{13,9},{2,6},{6,2},{1... | collective-permute-start | bytes 393224 | tf_op jit(solution)/shard_map/ppermute | solution.py:343
  30.7 1.0 collective-permute-start.7
  31.7 1.4 %collective-permute-start.8 = (bf16[32,2048]{1,0:T(8,128)(2,1)S(1)}, bf16[32,2048]{1,0:T(8,128)(2,1)S(1)}, u32[]{:S(2)}, u32[]{:S(2)}) collective-permute-start(bf16[32,2048]{1,0:T(8,128)(2,1)S(1)} %shard_map.104.refs_0_), channel_id=1, source_target_pairs={{0,12},{4,8},{8,4},{12,0},{1,13},{5,9},{9,5},{13,1},{2,14},{6,10},... | collective-permute-start | bytes 393224 | tf_op jit(solution)/shard_map/ppermute | solution.py:343
  33.1 1.8 %collective-permute-done.6.refs_1_ = bf16[32,2048]{1,0:T(8,128)(2,1)S(1)} collective-permute-done((bf16[32,2048]{1,0:T(8,128)(2,1)S(1)}, bf16[32,2048]{1,0:T(8,128)(2,1)S(1)}, u32[]{:S(2)}, u32[]{:S(2)}) %collective-permute-start.6) | collective-permute-done | bytes 131104 | tf_op jit(solution)/shard_map/ppermute | solution.py:343
  35.0 7.4 %collective-permute-done.7.refs_2_ = bf16[32,2048]{1,0:T(8,128)(2,1)S(1)} collective-permute-done((bf16[32,2048]{1,0:T(8,128)(2,1)S(1)}, bf16[32,2048]{1,0:T(8,128)(2,1)S(1)}, u32[]{:S(2)}, u32[]{:S(2)}) %collective-permute-start.7) | collective-permute-done | bytes 131104 | tf_op jit(solution)/shard_map/ppermute | solution.py:343
  42.4 1.8 %shard_map.105 = (f32[64,2048]{1,0:T(8,128)S(1)}, bf16[64,2048]{1,0:T(8,128)(2,1)S(1)}) custom-call(s32[12]{0:T(128)S(1)} %concatenate.3.meta_ref, bf16[32,2048]{1,0:T(8,128)(2,1)S(1)} %shard_map.104.refs_0_, bf16[32,2048]{1,0:T(8,128)(2,1)S(1)} %collective-permute-done.6.refs_1_, bf16[32,2048]{1,0:T(8,128)(2,1)S(1)} %collective-permute-done.7.refs_2_, ...), custom_call_target="tpu_custom_call" | custom-call | flops 6000000000 | bytes 9699376 | tf_op jit(solution)/shard_map/pallas_call | solution.py:37
  44.3 1.5 %collective-permute-done.9.got_ref = bf16[64,2048]{1,0:T(8,128)(2,1)S(1)} collective-permute-done((bf16[64,2048]{1,0:T(8,128)(2,1)S(1)}, bf16[64,2048]{1,0:T(8,128)(2,1)S(1)}, u32[]{:S(2)}, u32[]{:S(2)}) %collective-permute-start.9) | collective-permute-done | bytes 262176 | tf_op jit(solution)/shard_map/ppermute | solution.py:339
  45.9 0.6 shard_map.106
  46.5 1.6 %collective-permute-start.10 = (bf16[32,2048]{1,0:T(8,128)(2,1)S(1)}, bf16[32,2048]{1,0:T(8,128)(2,1)S(1)}, u32[]{:S(2)}, u32[]{:S(2)}) collective-permute-start(bf16[32,2048]{1,0:T(8,128)(2,1)S(1)} %get-tuple-element.41), channel_id=1, source_target_pairs={{0,2},{2,0},{1,3},{3,1},{4,6},{6,4},{5,7},{7,5},{8,10},{10,8},{9,1... | collective-permute-start | bytes 393224 | tf_op jit(solution)/shard_map/ppermute | solution.py:339
  48.1 4.0 %collective-permute-done.10.got_ref = bf16[32,2048]{1,0:T(8,128)(2,1)S(1)} collective-permute-done((bf16[32,2048]{1,0:T(8,128)(2,1)S(1)}, bf16[32,2048]{1,0:T(8,128)(2,1)S(1)}, u32[]{:S(2)}, u32[]{:S(2)}) %collective-permute-start.10) | collective-permute-done | bytes 131104 | tf_op jit(solution)/shard_map/ppermute | solution.py:339
  52.2 0.8 collective-permute-start.11
  53.0 3.5 %collective-permute-start.12 = (bf16[32,2048]{1,0:T(8,128)(2,1)S(1)}, bf16[32,2048]{1,0:T(8,128)(2,1)S(1)}, u32[]{:S(2)}, u32[]{:S(2)}) collective-permute-start(bf16[32,2048]{1,0:T(8,128)(2,1)S(1)} %shard_map.107), channel_id=1, source_target_pairs={{0,4},{1,0},{2,12},{3,8},{4,5},{5,1},{6,13},{7,9},{8,6},{9,2},{10,... | collective-permute-start | bytes 393224 | tf_op jit(solution)/shard_map/ppermute | solution.py:428
  56.5 2.8 %collective-permute-start.13 = (bf16[32,2048]{1,0:T(8,128)(2,1)S(1)}, bf16[32,2048]{1,0:T(8,128)(2,1)S(1)}, u32[]{:S(2)}, u32[]{:S(2)}) collective-permute-start(bf16[32,2048]{1,0:T(8,128)(2,1)S(1)} %shard_map.107), channel_id=1, source_target_pairs={{0,8},{1,12},{2,0},{3,4},{4,9},{5,13},{6,1},{7,5},{8,10},{9,14},{1... | collective-permute-start | bytes 393224 | tf_op jit(solution)/shard_map/ppermute | solution.py:428
  59.3 0.7 shard_map.108
  60.0 0.7 shard_map.109
  60.6 6.0 %collective-permute-done.13.piece_ref = bf16[32,2048]{1,0:T(8,128)(2,1)S(1)} collective-permute-done((bf16[32,2048]{1,0:T(8,128)(2,1)S(1)}, bf16[32,2048]{1,0:T(8,128)(2,1)S(1)}, u32[]{:S(2)}, u32[]{:S(2)}) %collective-permute-start.13) | collective-permute-done | bytes 131104 | tf_op jit(solution)/shard_map/ppermute | solution.py:428
  66.6 0.7 shard_map.110
  67.3 0.7 shard_map.111
  68.0 3.0 %shard_map.112 = (f32[64,3712]{1,0:T(8,128)S(1)}, bf16[64,3840]{1,0:T(8,128)(2,1)S(1)}, bf16[128,2048]{1,0:T(8,128)(2,1)S(1)}) custom-call(s32[12]{0:T(128)S(1)} %concatenate.3.meta_ref, bf16[32,2048]{1,0:T(8,128)(2,1)S(1)} %get-tuple-element.42.refs_0_, bf16[32,2048]{1,0:T(8,128)(2,1)S(1)} %get-tuple-element.43.refs_1_, ...), custom_call_target="tpu_custom_call" | custom-call | flops 3000000000 | bytes 31916080 | tf_op jit(solution)/shard_map/pallas_call | solution.py:37
  71.1 2.2 %shard_map.115 = (f32[64,3584]{1,0:T(8,128)S(1)}, bf16[64,3584]{1,0:T(8,128)(2,1)S(1)}) custom-call(bf16[128,2048]{1,0:T(8,128)(2,1)S(1)} %get-tuple-element.55.rows_ref, bf16[2048,3584]{1,0:T(8,128)(2,1)S(1)} %bitcast.7, bf16[2048,3584]{1,0:T(8,128)(2,1)S(1)} %bitcast.9), custom_call_target="tpu_custom_call" | custom-call | flops 3000000000 | bytes 31260672 | tf_op jit(solution)/shard_map/pallas_call | solution.py:37
  73.3 0.6 collective-permute-start.17
  73.8 0.7 shard_map.113
  74.5 6.2 %collective-permute-start.16 = (bf16[32,3840]{1,0:T(8,128)(2,1)S(1)}, bf16[32,3840]{1,0:T(8,128)(2,1)S(1)}, u32[]{:S(2)}, u32[]{:S(2)}) collective-permute-start(bf16[32,3840]{1,0:T(8,128)(2,1)S(1)} %get-tuple-element.53), channel_id=1, source_target_pairs={{0,2},{2,0},{1,3},{3,1},{4,6},{6,4},{5,7},{7,5},{8,10},{10,8},{9,1... | collective-permute-start | bytes 737288 | tf_op jit(solution)/shard_map/ppermute | solution.py:339
  80.7 0.6 shard_map.116
  81.4 0.8 collective-permute-start.18
  82.1 5.4 %collective-permute-done.16.got_ref = bf16[32,3840]{1,0:T(8,128)(2,1)S(1)} collective-permute-done((bf16[32,3840]{1,0:T(8,128)(2,1)S(1)}, bf16[32,3840]{1,0:T(8,128)(2,1)S(1)}, u32[]{:S(2)}, u32[]{:S(2)}) %collective-permute-start.16) | collective-permute-done | bytes 245792 | tf_op jit(solution)/shard_map/ppermute | solution.py:339
  87.7 2.1 %collective-permute-start.23 = (bf16[32,1792]{1,0:T(8,128)(2,1)S(1)}, bf16[32,1792]{1,0:T(8,128)(2,1)S(1)}, u32[]{:S(2)}, u32[]{:S(2)}) collective-permute-start(bf16[32,1792]{1,0:T(8,128)(2,1)S(1)} %get-tuple-element.60.refs_0_), channel_id=1, source_target_pairs={{0,2},{2,0},{1,3},{3,1},{4,6},{6,4},{5,7},{7,5},{8,10},{10,8},{9,1... | collective-permute-start | bytes 344072 | tf_op jit(solution)/shard_map/ppermute | solution.py:339
  89.7 2.7 %collective-permute-done.18.got_ref = bf16[32,3584]{1,0:T(8,128)(2,1)S(1)} collective-permute-done((bf16[32,3584]{1,0:T(8,128)(2,1)S(1)}, bf16[32,3584]{1,0:T(8,128)(2,1)S(1)}, u32[]{:S(2)}, u32[]{:S(2)}) %collective-permute-start.18) | collective-permute-done | bytes 229408 | tf_op jit(solution)/shard_map/ppermute | solution.py:339
  92.6 2.1 %collective-permute-start.20 = (bf16[32,1792]{1,0:T(8,128)(2,1)S(1)}, bf16[32,1792]{1,0:T(8,128)(2,1)S(1)}, u32[]{:S(2)}, u32[]{:S(2)}) collective-permute-start(bf16[32,1792]{1,0:T(8,128)(2,1)S(1)} %shard_map.117.refs_0_), channel_id=1, source_target_pairs={{0,2},{2,0},{1,3},{3,1},{4,6},{6,4},{5,7},{7,5},{8,10},{10,8},{9,1... | collective-permute-start | bytes 344072 | tf_op jit(solution)/shard_map/ppermute | solution.py:339
  95.2 2.3 %collective-permute-done.20.refs_2_ = bf16[32,1792]{1,0:T(8,128)(2,1)S(1)} collective-permute-done((bf16[32,1792]{1,0:T(8,128)(2,1)S(1)}, bf16[32,1792]{1,0:T(8,128)(2,1)S(1)}, u32[]{:S(2)}, u32[]{:S(2)}) %collective-permute-start.20) | collective-permute-done | bytes 114720 | tf_op jit(solution)/shard_map/ppermute | solution.py:339
  97.5 1.7 %shard_map.118.refs_5_ = f32[128,2048]{1,0:T(8,128)S(1)} custom-call(s32[12]{0:T(128)S(1)} %concatenate.3.meta_ref, bf16[32,1792]{1,0:T(8,128)(2,1)S(1)} %get-tuple-element.60.refs_0_, bf16[32,1792]{1,0:T(8,128)(2,1)S(1)} %collective-permute-done.22.refs_1_, bf16[32,1792]{1,0:T(8,128)(2,1)S(1)} %collective-permute-done.23.refs_2_, ...), custom_call_target="tpu_custom_call" | custom-call | flops 3000000000 | bytes 16187440 | tf_op jit(solution)/shard_map/pallas_call | solution.py:37
  99.2 1.7 %shard_map.119 = (f32[32,2048]{1,0:T(8,128)S(1)}, bf16[32,2048]{1,0:T(8,128)(2,1)S(1)}, bf16[32,2048]{1,0:T(8,128)(2,1)S(1)}, bf16[32,2048]{1,0:T(8,128)(2,1)S(1)}) custom-call(s32[12]{0:T(128)S(1)} %concatenate.3.meta_ref, bf16[32,1792]{1,0:T(8,128)(2,1)S(1)} %shard_map.117.refs_0_, bf16[32,1792]{1,0:T(8,128)(2,1)S(1)} %collective-permute-done.19.refs_1_, ...), custom_call_target="tpu_custom_call" | custom-call | flops 3000000000 | bytes 16842800 | tf_op jit(solution)/shard_map/pallas_call | solution.py:37
  100.9 3.1 %collective-permute-start.25 = (bf16[32,2048]{1,0:T(8,128)(2,1)S(1)}, bf16[32,2048]{1,0:T(8,128)(2,1)S(1)}, u32[]{:S(2)}, u32[]{:S(2)}) collective-permute-start(bf16[32,2048]{1,0:T(8,128)(2,1)S(1)} %get-tuple-element.62), channel_id=1, source_target_pairs={{0,12},{4,8},{8,4},{12,0},{1,13},{5,9},{9,5},{13,1},{2,14},{6,10},... | collective-permute-start | bytes 393224 | tf_op jit(solution)/shard_map/ppermute | solution.py:343
  104.0 1.4 %collective-permute-start.27 = (bf16[32,2048]{1,0:T(8,128)(2,1)S(1)}, bf16[32,2048]{1,0:T(8,128)(2,1)S(1)}, u32[]{:S(2)}, u32[]{:S(2)}) collective-permute-start(bf16[32,2048]{1,0:T(8,128)(2,1)S(1)} %get-tuple-element.64), channel_id=1, source_target_pairs={{0,4},{4,0},{8,12},{12,8},{1,5},{5,1},{9,13},{13,9},{2,6},{6,2},{1... | collective-permute-start | bytes 393224 | tf_op jit(solution)/shard_map/ppermute | solution.py:343
  105.4 3.9 %collective-permute-done.25.refs_0_ = bf16[32,2048]{1,0:T(8,128)(2,1)S(1)} collective-permute-done((bf16[32,2048]{1,0:T(8,128)(2,1)S(1)}, bf16[32,2048]{1,0:T(8,128)(2,1)S(1)}, u32[]{:S(2)}, u32[]{:S(2)}) %collective-permute-start.25) | collective-permute-done | bytes 131104 | tf_op jit(solution)/shard_map/ppermute | solution.py:343
  109.3 6.6 %collective-permute-done.26.refs_1_ = bf16[32,2048]{1,0:T(8,128)(2,1)S(1)} collective-permute-done((bf16[32,2048]{1,0:T(8,128)(2,1)S(1)}, bf16[32,2048]{1,0:T(8,128)(2,1)S(1)}, u32[]{:S(2)}, u32[]{:S(2)}) %collective-permute-start.26) | collective-permute-done | bytes 131104 | tf_op jit(solution)/shard_map/ppermute | solution.py:343
  115.9 0.8 shard_map.120
  (66 shorter events, 1.6 us)
Async XLA Ops:
  0.0 9.0 %collective-permute-start = (bf16[32,2048]{1,0:T(8,128)(2,1)}, bf16[32,2048]{1,0:T(8,128)(2,1)S(1)}, u32[]{:S(2)}, u32[]{:S(2)}) collective-permute-start(bf16[32,2048]{1,0:T(8,128)(2,1)} %q_hbm.1), channel_id=1, source_target_pairs={{0,4},{4,0},{8,12},{12,8},{1,5},{5,1},{9,13},{13,9},{2,6},{6,2},{1... | collective-permute-start | bytes 393224 | tf_op jit(solution)/shard_map/ppermute | solution.py:343
  3.1 13.1 %collective-permute-start.2 = (bf16[32,2048]{1,0:T(8,128)(2,1)}, bf16[32,2048]{1,0:T(8,128)(2,1)S(1)}, u32[]{:S(2)}, u32[]{:S(2)}) collective-permute-start(bf16[32,2048]{1,0:T(8,128)(2,1)} %q_hbm.1), channel_id=1, source_target_pairs={{0,8},{4,12},{8,0},{12,4},{1,9},{5,13},{9,1},{13,5},{2,10},{6,14},... | collective-permute-start | bytes 393224 | tf_op jit(solution)/shard_map/ppermute | solution.py:343
  5.6 12.0 %collective-permute-start.4 = (bf16[32,2048]{1,0:T(8,128)(2,1)}, bf16[32,2048]{1,0:T(8,128)(2,1)S(1)}, u32[]{:S(2)}, u32[]{:S(2)}) collective-permute-start(bf16[32,2048]{1,0:T(8,128)(2,1)} %q_hbm.1), channel_id=1, source_target_pairs={{0,12},{4,8},{8,4},{12,0},{1,13},{5,9},{9,5},{13,1},{2,14},{6,10},... | collective-permute-start | bytes 393224 | tf_op jit(solution)/shard_map/ppermute | solution.py:343
  10.3 32.1 %slice-start.12 = ((s8[8388608]{0:T(1024)(128)(4,1)}), s8[4194304]{0:T(1024)(128)(4,1)S(1)}, s32[]{:S(2)}) async-start(s8[8388608]{0:T(1024)(128)(4,1)} %bitcast.16), calls=%async_computation.12 | async-start | bytes 8388608
  10.3 11.0 %collective-permute-start.1 = (bf16[32,2176]{1,0:T(8,128)(2,1)S(1)}, bf16[32,2176]{1,0:T(8,128)(2,1)S(1)}, u32[]{:S(2)}, u32[]{:S(2)}) collective-permute-start(bf16[32,2176]{1,0:T(8,128)(2,1)S(1)} %shard_map.101), channel_id=1, source_target_pairs={{0,4},{4,0},{8,12},{12,8},{1,5},{5,1},{9,13},{13,9},{2,6},{6,2},{1... | collective-permute-start | bytes 417800 | tf_op jit(solution)/shard_map/ppermute | solution.py:343
  17.5 24.9 %slice-start.13 = ((s8[8388608]{0:T(1024)(128)(4,1)}), s8[4194304]{0:T(1024)(128)(4,1)S(1)}, s32[]{:S(2)}) async-start(s8[8388608]{0:T(1024)(128)(4,1)} %bitcast.16), calls=%async_computation.13 | async-start | bytes 8388608
  17.6 10.5 %collective-permute-start.3 = (bf16[32,2176]{1,0:T(8,128)(2,1)S(1)}, bf16[32,2176]{1,0:T(8,128)(2,1)S(1)}, u32[]{:S(2)}, u32[]{:S(2)}) collective-permute-start(bf16[32,2176]{1,0:T(8,128)(2,1)S(1)} %shard_map.102), channel_id=1, source_target_pairs={{0,8},{4,12},{8,0},{12,4},{1,9},{5,13},{9,1},{13,5},{2,10},{6,14},... | collective-permute-start | bytes 417800 | tf_op jit(solution)/shard_map/ppermute | solution.py:343
  19.0 9.1 %collective-permute-start.5 = (bf16[32,2176]{1,0:T(8,128)(2,1)S(1)}, bf16[32,2176]{1,0:T(8,128)(2,1)S(1)}, u32[]{:S(2)}, u32[]{:S(2)}) collective-permute-start(bf16[32,2176]{1,0:T(8,128)(2,1)S(1)} %shard_map.103), channel_id=1, source_target_pairs={{0,12},{4,8},{8,4},{12,0},{1,13},{5,9},{9,5},{13,1},{2,14},{6,10},... | collective-permute-start | bytes 417800 | tf_op jit(solution)/shard_map/ppermute | solution.py:343
  28.6 6.4 %collective-permute-start.6 = (bf16[32,2048]{1,0:T(8,128)(2,1)S(1)}, bf16[32,2048]{1,0:T(8,128)(2,1)S(1)}, u32[]{:S(2)}, u32[]{:S(2)}) collective-permute-start(bf16[32,2048]{1,0:T(8,128)(2,1)S(1)} %shard_map.104.refs_0_), channel_id=1, source_target_pairs={{0,4},{4,0},{8,12},{12,8},{1,5},{5,1},{9,13},{13,9},{2,6},{6,2},{1... | collective-permute-start | bytes 393224 | tf_op jit(solution)/shard_map/ppermute | solution.py:343
  30.7 11.7 %collective-permute-start.7 = (bf16[32,2048]{1,0:T(8,128)(2,1)S(1)}, bf16[32,2048]{1,0:T(8,128)(2,1)S(1)}, u32[]{:S(2)}, u32[]{:S(2)}) collective-permute-start(bf16[32,2048]{1,0:T(8,128)(2,1)S(1)} %shard_map.104.refs_0_), channel_id=1, source_target_pairs={{0,8},{4,12},{8,0},{12,4},{1,9},{5,13},{9,1},{13,5},{2,10},{6,14},... | collective-permute-start | bytes 393224 | tf_op jit(solution)/shard_map/ppermute | solution.py:343
  31.7 10.7 %collective-permute-start.8 = (bf16[32,2048]{1,0:T(8,128)(2,1)S(1)}, bf16[32,2048]{1,0:T(8,128)(2,1)S(1)}, u32[]{:S(2)}, u32[]{:S(2)}) collective-permute-start(bf16[32,2048]{1,0:T(8,128)(2,1)S(1)} %shard_map.104.refs_0_), channel_id=1, source_target_pairs={{0,12},{4,8},{8,4},{12,0},{1,13},{5,9},{9,5},{13,1},{2,14},{6,10},... | collective-permute-start | bytes 393224 | tf_op jit(solution)/shard_map/ppermute | solution.py:343
  44.3 7.8 %copy-start.1 = (bf16[32,2048]{1,0:T(8,128)(2,1)S(1)}, bf16[32,2048]{1,0:T(8,128)(2,1)}, u32[]{:S(2)}) copy-start(bf16[32,2048]{1,0:T(8,128)(2,1)} %stream_ref.1) | copy-start | bytes 393220
  44.3 1.6 %collective-permute-start.9 = (bf16[64,2048]{1,0:T(8,128)(2,1)S(1)}, bf16[64,2048]{1,0:T(8,128)(2,1)S(1)}, u32[]{:S(2)}, u32[]{:S(2)}) collective-permute-start(bf16[64,2048]{1,0:T(8,128)(2,1)S(1)} %get-tuple-element.39), channel_id=1, source_target_pairs={{0,1},{1,0},{2,3},{3,2},{4,5},{5,4},{6,7},{7,6},{8,9},{9,8},{10,11... | collective-permute-start | bytes 786440 | tf_op jit(solution)/shard_map/ppermute | solution.py:339
  45.9 22.1 %slice-start = ((s8[14680064]{0:T(1024)(128)(4,1)}), s8[4194304]{0:T(1024)(128)(4,1)S(1)}, s32[]{:S(2)}) async-start(s8[14680064]{0:T(1024)(128)(4,1)} %bitcast.6), calls=%async_computation | async-start | bytes 8388608
  45.9 22.1 %slice-start.1 = ((s8[14680064]{0:T(1024)(128)(4,1)}), s8[4194304]{0:T(1024)(128)(4,1)S(1)}, s32[]{:S(2)}) async-start(s8[14680064]{0:T(1024)(128)(4,1)} %bitcast.6), calls=%async_computation.1 | async-start | bytes 8388608
  45.9 22.1 %slice-start.4 = ((s8[14680064]{0:T(1024)(128)(4,1)}), s8[2097152]{0:T(1024)(128)(4,1)S(1)}, s32[]{:S(2)}) async-start(s8[14680064]{0:T(1024)(128)(4,1)} %bitcast.8), calls=%async_computation.4 | async-start | bytes 4194304
  45.9 22.1 %slice-start.5 = ((s8[14680064]{0:T(1024)(128)(4,1)}), s8[4194304]{0:T(1024)(128)(4,1)S(1)}, s32[]{:S(2)}) async-start(s8[14680064]{0:T(1024)(128)(4,1)} %bitcast.8), calls=%async_computation.5 | async-start | bytes 8388608
  46.5 12.8 %copy-start = (f32[8192]{0:T(1024)S(1)}, f32[8192]{0:T(1024)}, u32[]{:S(2)}) copy-start(f32[8192]{0:T(1024)} %param.16) | copy-start | bytes 98308
  46.5 5.6 %collective-permute-start.10 = (bf16[32,2048]{1,0:T(8,128)(2,1)S(1)}, bf16[32,2048]{1,0:T(8,128)(2,1)S(1)}, u32[]{:S(2)}, u32[]{:S(2)}) collective-permute-start(bf16[32,2048]{1,0:T(8,128)(2,1)S(1)} %get-tuple-element.41), channel_id=1, source_target_pairs={{0,2},{2,0},{1,3},{3,1},{4,6},{6,4},{5,7},{7,5},{8,10},{10,8},{9,1... | collective-permute-start | bytes 393224 | tf_op jit(solution)/shard_map/ppermute | solution.py:339
  52.1 15.9 %slice-start.2 = ((s8[14680064]{0:T(1024)(128)(4,1)}), s8[4194304]{0:T(1024)(128)(4,1)S(1)}, s32[]{:S(2)}) async-start(s8[14680064]{0:T(1024)(128)(4,1)} %bitcast.6), calls=%async_computation.2 | async-start | bytes 8388608
  52.1 15.9 %slice-start.3 = ((s8[14680064]{0:T(1024)(128)(4,1)}), s8[2097152]{0:T(1024)(128)(4,1)S(1)}, s32[]{:S(2)}) async-start(s8[14680064]{0:T(1024)(128)(4,1)} %bitcast.6), calls=%async_computation.3 | async-start | bytes 4194304
  52.1 15.9 %slice-start.6 = ((s8[14680064]{0:T(1024)(128)(4,1)}), s8[4194304]{0:T(1024)(128)(4,1)S(1)}, s32[]{:S(2)}) async-start(s8[14680064]{0:T(1024)(128)(4,1)} %bitcast.8), calls=%async_computation.6 | async-start | bytes 8388608
  52.1 15.9 %slice-start.7 = ((s8[14680064]{0:T(1024)(128)(4,1)}), s8[4194304]{0:T(1024)(128)(4,1)S(1)}, s32[]{:S(2)}) async-start(s8[14680064]{0:T(1024)(128)(4,1)} %bitcast.8), calls=%async_computation.7 | async-start | bytes 8388608
  52.2 7.1 %collective-permute-start.11 = (bf16[32,2048]{1,0:T(8,128)(2,1)S(1)}, bf16[32,2048]{1,0:T(8,128)(2,1)S(1)}, u32[]{:S(2)}, u32[]{:S(2)}) collective-permute-start(bf16[32,2048]{1,0:T(8,128)(2,1)S(1)} %shard_map.107), channel_id=1, source_target_pairs={{0,0},{1,4},{2,8},{3,12},{4,1},{5,5},{6,9},{7,13},{8,2},{9,6},{10,... | collective-permute-start | bytes 393224 | tf_op jit(solution)/shard_map/ppermute | solution.py:428
  53.0 7.0 %collective-permute-start.12 = (bf16[32,2048]{1,0:T(8,128)(2,1)S(1)}, bf16[32,2048]{1,0:T(8,128)(2,1)S(1)}, u32[]{:S(2)}, u32[]{:S(2)}) collective-permute-start(bf16[32,2048]{1,0:T(8,128)(2,1)S(1)} %shard_map.107), channel_id=1, source_target_pairs={{0,4},{1,0},{2,12},{3,8},{4,5},{5,1},{6,13},{7,9},{8,6},{9,2},{10,... | collective-permute-start | bytes 393224 | tf_op jit(solution)/shard_map/ppermute | solution.py:428
  56.5 10.1 %collective-permute-start.13 = (bf16[32,2048]{1,0:T(8,128)(2,1)S(1)}, bf16[32,2048]{1,0:T(8,128)(2,1)S(1)}, u32[]{:S(2)}, u32[]{:S(2)}) collective-permute-start(bf16[32,2048]{1,0:T(8,128)(2,1)S(1)} %shard_map.107), channel_id=1, source_target_pairs={{0,8},{1,12},{2,0},{3,4},{4,9},{5,13},{6,1},{7,5},{8,10},{9,14},{1... | collective-permute-start | bytes 393224 | tf_op jit(solution)/shard_map/ppermute | solution.py:428
  59.3 8.0 %collective-permute-start.14 = (bf16[32,2048]{1,0:T(8,128)(2,1)S(1)}, bf16[32,2048]{1,0:T(8,128)(2,1)S(1)}, u32[]{:S(2)}, u32[]{:S(2)}) collective-permute-start(bf16[32,2048]{1,0:T(8,128)(2,1)S(1)} %shard_map.107), channel_id=1, source_target_pairs={{0,12},{1,8},{2,4},{3,0},{4,13},{5,9},{6,5},{7,1},{8,14},{9,10},{1... | collective-permute-start | bytes 393224 | tf_op jit(solution)/shard_map/ppermute | solution.py:428
  71.0 2.8 %collective-permute-start.15 = (bf16[64,3840]{1,0:T(8,128)(2,1)S(1)}, bf16[64,3840]{1,0:T(8,128)(2,1)S(1)}, u32[]{:S(2)}, u32[]{:S(2)}) collective-permute-start(bf16[64,3840]{1,0:T(8,128)(2,1)S(1)} %get-tuple-element.51), channel_id=1, source_target_pairs={{0,1},{1,0},{2,3},{3,2},{4,5},{5,4},{6,7},{7,6},{8,9},{9,8},{10,11... | collective-permute-start | bytes 1474568 | tf_op jit(solution)/shard_map/ppermute | solution.py:339
  73.3 7.5 %collective-permute-start.17 = (bf16[64,3584]{1,0:T(8,128)(2,1)S(1)}, bf16[64,3584]{1,0:T(8,128)(2,1)S(1)}, u32[]{:S(2)}, u32[]{:S(2)}) collective-permute-start(bf16[64,3584]{1,0:T(8,128)(2,1)S(1)} %get-tuple-element.57), channel_id=1, source_target_pairs={{0,1},{1,0},{2,3},{3,2},{4,5},{5,4},{6,7},{7,6},{8,9},{9,8},{10,11... | collective-permute-start | bytes 1376264 | tf_op jit(solution)/shard_map/ppermute | solution.py:339
  74.5 13.1 %collective-permute-start.16 = (bf16[32,3840]{1,0:T(8,128)(2,1)S(1)}, bf16[32,3840]{1,0:T(8,128)(2,1)S(1)}, u32[]{:S(2)}, u32[]{:S(2)}) collective-permute-start(bf16[32,3840]{1,0:T(8,128)(2,1)S(1)} %get-tuple-element.53), channel_id=1, source_target_pairs={{0,2},{2,0},{1,3},{3,1},{4,6},{6,4},{5,7},{7,5},{8,10},{10,8},{9,1... | collective-permute-start | bytes 737288 | tf_op jit(solution)/shard_map/ppermute | solution.py:339
  80.7 16.7 %slice-start.8 = ((s8[14680064]{0:T(1024)(128)(4,1)}), s8[4194304]{0:T(1024)(128)(4,1)S(1)}, s32[]{:S(2)}) async-start(s8[14680064]{0:T(1024)(128)(4,1)} %bitcast.10), calls=%async_computation.8 | async-start | bytes 8388608
  80.7 16.7 %slice-start.9 = ((s8[14680064]{0:T(1024)(128)(4,1)}), s8[4194304]{0:T(1024)(128)(4,1)S(1)}, s32[]{:S(2)}) async-start(s8[14680064]{0:T(1024)(128)(4,1)} %bitcast.10), calls=%async_computation.9 | async-start | bytes 8388608
  81.4 11.1 %collective-permute-start.18 = (bf16[32,3584]{1,0:T(8,128)(2,1)S(1)}, bf16[32,3584]{1,0:T(8,128)(2,1)S(1)}, u32[]{:S(2)}, u32[]{:S(2)}) collective-permute-start(bf16[32,3584]{1,0:T(8,128)(2,1)S(1)} %get-tuple-element.59), channel_id=1, source_target_pairs={{0,2},{2,0},{1,3},{3,1},{4,6},{6,4},{5,7},{7,5},{8,10},{10,8},{9,1... | collective-permute-start | bytes 688136 | tf_op jit(solution)/shard_map/ppermute | solution.py:339
  87.5 9.9 %slice-start.10 = ((s8[14680064]{0:T(1024)(128)(4,1)}), s8[4194304]{0:T(1024)(128)(4,1)S(1)}, s32[]{:S(2)}) async-start(s8[14680064]{0:T(1024)(128)(4,1)} %bitcast.10), calls=%async_computation.10 | async-start | bytes 8388608
  87.7 7.0 %collective-permute-start.23 = (bf16[32,1792]{1,0:T(8,128)(2,1)S(1)}, bf16[32,1792]{1,0:T(8,128)(2,1)S(1)}, u32[]{:S(2)}, u32[]{:S(2)}) collective-permute-start(bf16[32,1792]{1,0:T(8,128)(2,1)S(1)} %get-tuple-element.60.refs_0_), channel_id=1, source_target_pairs={{0,2},{2,0},{1,3},{3,1},{4,6},{6,4},{5,7},{7,5},{8,10},{10,8},{9,1... | collective-permute-start | bytes 344072 | tf_op jit(solution)/shard_map/ppermute | solution.py:339
  92.4 5.0 %slice-start.11 = ((s8[14680064]{0:T(1024)(128)(4,1)}), s8[2097152]{0:T(1024)(128)(4,1)S(1)}, s32[]{:S(2)}) async-start(s8[14680064]{0:T(1024)(128)(4,1)} %bitcast.10), calls=%async_computation.11 | async-start | bytes 4194304
  92.6 4.9 %collective-permute-start.20 = (bf16[32,1792]{1,0:T(8,128)(2,1)S(1)}, bf16[32,1792]{1,0:T(8,128)(2,1)S(1)}, u32[]{:S(2)}, u32[]{:S(2)}) collective-permute-start(bf16[32,1792]{1,0:T(8,128)(2,1)S(1)} %shard_map.117.refs_0_), channel_id=1, source_target_pairs={{0,2},{2,0},{1,3},{3,1},{4,6},{6,4},{5,7},{7,5},{8,10},{10,8},{9,1... | collective-permute-start | bytes 344072 | tf_op jit(solution)/shard_map/ppermute | solution.py:339
  94.7 2.8 %collective-permute-start.22 = (bf16[32,1792]{1,0:T(8,128)(2,1)S(1)}, bf16[32,1792]{1,0:T(8,128)(2,1)S(1)}, u32[]{:S(2)}, u32[]{:S(2)}) collective-permute-start(bf16[32,1792]{1,0:T(8,128)(2,1)S(1)} %get-tuple-element.60.refs_0_), channel_id=1, source_target_pairs={{0,1},{1,0},{2,3},{3,2},{4,5},{5,4},{6,7},{7,6},{8,9},{9,8},{10,11... | collective-permute-start | bytes 344072 | tf_op jit(solution)/shard_map/ppermute | solution.py:339
  94.7 2.8 %collective-permute-start.24 = (bf16[32,1792]{1,0:T(8,128)(2,1)S(1)}, bf16[32,1792]{1,0:T(8,128)(2,1)S(1)}, u32[]{:S(2)}, u32[]{:S(2)}) collective-permute-start(bf16[32,1792]{1,0:T(8,128)(2,1)S(1)} %collective-permute-done.23.refs_2_), channel_id=1, source_target_pairs={{0,1},{1,0},{2,3},{3,2},{4,5},{5,4},{6,7},{7,6},{8,9},{9,8},{10,11... | collective-permute-start | bytes 344072 | tf_op jit(solution)/shard_map/ppermute | solution.py:339
  95.2 4.0 %collective-permute-start.19 = (bf16[32,1792]{1,0:T(8,128)(2,1)S(1)}, bf16[32,1792]{1,0:T(8,128)(2,1)S(1)}, u32[]{:S(2)}, u32[]{:S(2)}) collective-permute-start(bf16[32,1792]{1,0:T(8,128)(2,1)S(1)} %shard_map.117.refs_0_), channel_id=1, source_target_pairs={{0,1},{1,0},{2,3},{3,2},{4,5},{5,4},{6,7},{7,6},{8,9},{9,8},{10,11... | collective-permute-start | bytes 344072 | tf_op jit(solution)/shard_map/ppermute | solution.py:339
  97.4 1.8 %collective-permute-start.21 = (bf16[32,1792]{1,0:T(8,128)(2,1)S(1)}, bf16[32,1792]{1,0:T(8,128)(2,1)S(1)}, u32[]{:S(2)}, u32[]{:S(2)}) collective-permute-start(bf16[32,1792]{1,0:T(8,128)(2,1)S(1)} %collective-permute-done.20.refs_2_), channel_id=1, source_target_pairs={{0,1},{1,0},{2,3},{3,2},{4,5},{5,4},{6,7},{7,6},{8,9},{9,8},{10,11... | collective-permute-start | bytes 344072 | tf_op jit(solution)/shard_map/ppermute | solution.py:339
  100.9 8.3 %collective-permute-start.25 = (bf16[32,2048]{1,0:T(8,128)(2,1)S(1)}, bf16[32,2048]{1,0:T(8,128)(2,1)S(1)}, u32[]{:S(2)}, u32[]{:S(2)}) collective-permute-start(bf16[32,2048]{1,0:T(8,128)(2,1)S(1)} %get-tuple-element.62), channel_id=1, source_target_pairs={{0,12},{4,8},{8,4},{12,0},{1,13},{5,9},{9,5},{13,1},{2,14},{6,10},... | collective-permute-start | bytes 393224 | tf_op jit(solution)/shard_map/ppermute | solution.py:343
  104.0 11.8 %collective-permute-start.26 = (bf16[32,2048]{1,0:T(8,128)(2,1)S(1)}, bf16[32,2048]{1,0:T(8,128)(2,1)S(1)}, u32[]{:S(2)}, u32[]{:S(2)}) collective-permute-start(bf16[32,2048]{1,0:T(8,128)(2,1)S(1)} %get-tuple-element.63), channel_id=1, source_target_pairs={{0,8},{4,12},{8,0},{12,4},{1,9},{5,13},{9,1},{13,5},{2,10},{6,14},... | collective-permute-start | bytes 393224 | tf_op jit(solution)/shard_map/ppermute | solution.py:343
  104.0 11.8 %collective-permute-start.27 = (bf16[32,2048]{1,0:T(8,128)(2,1)S(1)}, bf16[32,2048]{1,0:T(8,128)(2,1)S(1)}, u32[]{:S(2)}, u32[]{:S(2)}) collective-permute-start(bf16[32,2048]{1,0:T(8,128)(2,1)S(1)} %get-tuple-element.64), channel_id=1, source_target_pairs={{0,4},{4,0},{8,12},{12,8},{1,5},{5,1},{9,13},{13,9},{2,6},{6,2},{1... | collective-permute-start | bytes 393224 | tf_op jit(solution)/shard_map/ppermute | solution.py:343
